TPU v7x, 32 devices: a whole 2x2x4 slice. The times are simulated.
32 devices in a mesh: freq: 2 (over x), facet: 16 (over z, y, core).
Axes of the slice: x: 2, y: 2, z: 4, core: 2. Of those that a mesh axis runs over, the one named last changes fastest.
Arguments:
- model_image: float32 [128, 2048], P('facet'), may hold values from -6 to 6
- visibilities: float32 [2, 8192], P(None, ('freq', 'facet')), may hold values from -6 to 6
- kernel_u: float32 [16, 8192], P(None, ('freq', 'facet')), may hold values from -1.5 to 1.5
- kernel_v: float32 [16, 8192], P(None, ('freq', 'facet')), may hold values from -1.5 to 1.5
- owners: int32 [8192, 1], P(('freq', 'facet')), may hold values from 0 to 15; in each aligned block of 256 rows (0 to 255, 256 to 511, ...) at most 64 rows name the same one
- offsets: int32 [2, 8192], P(None, ('freq', 'facet')), may hold values from 0 to 48
- corners: int32 [2, 16, 2], P('freq'), may hold values from -8192 to 8128
Outputs:
- model_out: float32 [128, 2048], P('facet')
- residual_rows: float32 [2, 8192], P(None, ('freq', 'facet'))
Inputs may be any that keep to these rules, and one draw needn't show every extreme that they name: `owners`: within each device's 256 rows, at most 64 rows name one owner, a bound that some block reaches of them.
All inputs are finite; a program needn't handle non-finite values.
Results may differ from a plain program's by a relative error of at most 0.0045.
Values sent between devices are 32-bit elements; how exact they have to be, the bound alone decides.
No kernel may reach another device: no remote copies, remote signals or barrier semaphores. Data moves between devices by JAX's collectives and lax.ppermute only.
A program may use at most 64 MiB of HBM per device.

v0:
```python
import math

import jax
import jax.numpy as jnp
from jax import lax
from jax.sharding import PartitionSpec as P

GRID = 16384
FACET = 2048
FROWS = 8
SUB = 64
SUPPORT = 16
CYCLES = 2


exact_products = lax.Precision.HIGHEST
GAIN_STEP = 0.5


def phase_pair(freq_index, position):
    angle_value = jnp.mod(freq_index * position, GRID).astype(jnp.float32) * (2.0 * math.pi / GRID)
    return (jnp.cos(angle_value), jnp.sin(angle_value))


def column_table():
    columns = jnp.arange(FACET, dtype=jnp.int32)
    frequency = jnp.arange(SUB, dtype=jnp.int32)
    cos_t, sin_t = phase_pair(frequency[None, :], columns[:, None])
    return jnp.concatenate([cos_t, sin_t], axis=1)


def make_back(col_table):
    cos_t = col_table[:, :SUB].T
    sin_t = col_table[:, SUB:].T
    upper = jnp.concatenate([cos_t, sin_t], axis=1)
    lower = jnp.concatenate([-sin_t, cos_t], axis=1)
    return jnp.concatenate([upper, lower], axis=0)


def forward_part(images, facet_ids, u_start, v_start, col_table):
    amount = images.shape[0]
    columns = jnp.arange(FACET, dtype=jnp.int32)
    cos_u, sin_u = phase_pair(u_start, columns)
    real_mod = (images * cos_u).reshape(amount * FROWS, FACET).astype(jnp.bfloat16)
    imag_mod = (-images * sin_u).reshape(amount * FROWS, FACET).astype(jnp.bfloat16)
    table_half = col_table.astype(jnp.bfloat16)
    real_prod = jnp.dot(real_mod, table_half, preferred_element_type=jnp.float32).reshape(
        amount, FROWS, 2 * SUB
    )
    imag_prod = jnp.dot(imag_mod, table_half, preferred_element_type=jnp.float32).reshape(
        amount, FROWS, 2 * SUB
    )
    col_re = real_prod[..., :SUB] + imag_prod[..., SUB:]
    col_im = imag_prod[..., :SUB] - real_prod[..., SUB:]
    frequency = jnp.arange(SUB, dtype=jnp.int32)
    x_start = facet_ids % (GRID // FACET) * FACET - GRID // 2
    cos_x, sin_x = phase_pair(u_start + frequency[None, :], x_start[:, None])
    shift_re = col_re * cos_x[:, None, :] + col_im * sin_x[:, None, :]
    shift_im = col_im * cos_x[:, None, :] - col_re * sin_x[:, None, :]
    y_pos = (facet_ids // (GRID // FACET) * FACET - GRID // 2)[:, None] + jnp.arange(
        FROWS, dtype=jnp.int32
    )[None, :]
    cosine_vertical, sine_vertical = phase_pair(v_start + frequency[:, None, None], y_pos[None])
    grid_re = jnp.einsum(
        "bfr,fra->ba", cosine_vertical, shift_re, precision=exact_products
    ) + jnp.einsum("bfr,fra->ba", sine_vertical, shift_im, precision=exact_products)
    grid_im = jnp.einsum(
        "bfr,fra->ba", cosine_vertical, shift_im, precision=exact_products
    ) - jnp.einsum("bfr,fra->ba", sine_vertical, shift_re, precision=exact_products)
    return jnp.stack([grid_re, grid_im], axis=1)


def forward_sum(images, facet_ids, u_start, v_start, col_table):
    amount = images.shape[0]
    blocking = math.gcd(amount, 8)

    def forward_accumulate(running, pieces):
        return (running + forward_part(pieces[0], pieces[1], u_start, v_start, col_table), None)

    sectioned = images.reshape(amount // blocking, blocking, FROWS, FACET)
    sectioned_ids = facet_ids.reshape(amount // blocking, blocking)
    running, unused = lax.scan(
        forward_accumulate, jnp.zeros((SUB, 2, SUB), jnp.float32), (sectioned, sectioned_ids)
    )
    return running


def adjoint_part(blocks, u_starts, v_starts, facet_here, back_table):
    amount = blocks.shape[0]
    frequency = jnp.arange(SUB, dtype=jnp.int32)
    y_pos = facet_here // (GRID // FACET) * FACET - GRID // 2 + jnp.arange(FROWS, dtype=jnp.int32)
    cosine_vertical, sine_vertical = phase_pair(
        v_starts[:, None, None] + frequency[None, :, None], y_pos[None, None, :]
    )
    kernel_real = blocks[:, :, 0, :]
    kernel_imaginary = blocks[:, :, 1, :]
    row_real = jnp.einsum(
        "gil,gik->glk", cosine_vertical, kernel_real, precision=exact_products
    ) - jnp.einsum("gil,gik->glk", sine_vertical, kernel_imaginary, precision=exact_products)
    row_imaginary = jnp.einsum(
        "gil,gik->glk", cosine_vertical, kernel_imaginary, precision=exact_products
    ) + jnp.einsum("gil,gik->glk", sine_vertical, kernel_real, precision=exact_products)
    x_start = facet_here % (GRID // FACET) * FACET - GRID // 2
    cos_x, sin_x = phase_pair(u_starts[:, None] + frequency[None, :], x_start)
    shift_re = row_real * cos_x[:, None, :] - row_imaginary * sin_x[:, None, :]
    shift_im = row_imaginary * cos_x[:, None, :] + row_real * sin_x[:, None, :]
    joined = (
        jnp.concatenate([shift_re, shift_im], axis=2)
        .reshape(amount * FROWS, 2 * SUB)
        .astype(jnp.bfloat16)
    )
    both = jnp.dot(
        joined, back_table.astype(jnp.bfloat16), preferred_element_type=jnp.float32
    ).reshape(amount, FROWS, 2 * FACET)
    columns = jnp.arange(FACET, dtype=jnp.int32)
    cos_u, sin_u = phase_pair(u_starts[:, None], columns[None, :])
    return jnp.sum(
        both[..., :FACET] * cos_u[:, None, :] - both[..., FACET:] * sin_u[:, None, :], axis=0
    )


def adjoint_sum(blocks, corner_list, facet_here, back_table):
    amount = blocks.shape[0]
    blocking = math.gcd(amount, 8)

    def adjoint_accumulate(running, pieces):
        return (
            running
            + adjoint_part(pieces[0], pieces[1][:, 0], pieces[1][:, 1], facet_here, back_table),
            None,
        )

    sectioned = blocks.reshape(amount // blocking, blocking, SUB, 2, SUB)
    starts = corner_list.reshape(amount // blocking, blocking, 2)
    running, unused = lax.scan(
        adjoint_accumulate, jnp.zeros((FROWS, FACET), jnp.float32), (sectioned, starts)
    )
    return running


def slot_positions(owner_ids, capacity, owner_count):
    owner_hits = (owner_ids[:, None] == jnp.arange(owner_count, dtype=jnp.int32)[None, :]).astype(
        jnp.int32
    )
    before = jnp.cumsum(owner_hits, axis=0) - owner_hits
    return owner_ids * capacity + jnp.sum(before * owner_hits, axis=1)


def place_kernel(kernel, offset_row):
    row_ids = jnp.arange(SUB, dtype=jnp.int32)[:, None]
    placed = jnp.zeros((SUB, kernel.shape[1]), jnp.float32)
    for kernel_tap in range(SUPPORT):
        placed = placed + jnp.where(
            row_ids == offset_row[None, :] + kernel_tap, kernel[kernel_tap][None, :], 0.0
        )
    return placed


def predict_rows(grid_block, kern_u, kern_v):
    partial_rows = jnp.einsum("bpa,ar->bpr", grid_block, kern_u, precision=exact_products)
    return jnp.sum(kern_v[:, None, :] * partial_rows, axis=0)


def grid_rows(residual, kern_u, kern_v):
    return jnp.einsum(
        "br,par->bpa", kern_v, residual[:, None, :] * kern_u[None], precision=exact_products
    )


def on_device(model_image, visibilities, kernel_u, kernel_v, owners, offsets, corners):
    facet_count = lax.axis_size("facet")
    facet_here = lax.axis_index("facet")
    device_rows = owners.shape[0]
    capacity = 4 * device_rows // facet_count
    scale = 1.0 / math.sqrt(facet_count * FROWS * FACET)
    slot_index = slot_positions(owners[:, 0], capacity, facet_count)
    payload = jnp.concatenate(
        [visibilities, kernel_u, kernel_v, offsets.astype(jnp.float32)], axis=0
    )
    feature_rows = payload.shape[0]
    send_buffer = (
        jnp.zeros((feature_rows, facet_count * capacity), jnp.float32)
        .at[:, slot_index]
        .set(payload)
    )
    send_buffer = send_buffer.reshape(feature_rows, facet_count, capacity)
    arrived = lax.all_to_all(send_buffer, "facet", split_axis=1, concat_axis=1, tiled=True).reshape(
        feature_rows, facet_count * capacity
    )
    observed = arrived[0:2]
    kern_u = place_kernel(arrived[2 : 2 + SUPPORT], arrived[2 + 2 * SUPPORT].astype(jnp.int32))
    kern_v = place_kernel(
        arrived[2 + SUPPORT : 2 + 2 * SUPPORT], arrived[3 + 2 * SUPPORT].astype(jnp.int32)
    )
    corner_list = corners[0]
    own_corner = corner_list[facet_here]
    col_table = column_table()
    back_table = make_back(col_table)
    current = model_image
    residual = observed
    for major_cycle in range(CYCLES):
        gathered = lax.all_gather(current, "facet", axis=0, tiled=True)
        amount = gathered.shape[0] // FROWS
        facet_ids = jnp.arange(amount, dtype=jnp.int32)
        summed = forward_sum(
            gathered.reshape(amount, FROWS, FACET),
            facet_ids,
            own_corner[0],
            own_corner[1],
            col_table,
        )
        grid_block = scale * summed
        residual = observed - predict_rows(grid_block, kern_u, kern_v)
        gridded = grid_rows(residual, kern_u, kern_v)
        add_gathered = lax.all_gather(gridded, "facet", axis=0, tiled=True)
        add_amount = add_gathered.shape[0] // SUB
        dirty_image = scale * adjoint_sum(
            add_gathered.reshape(add_amount, SUB, 2, SUB), corner_list, facet_here, back_table
        )
        current = current + GAIN_STEP * lax.psum(dirty_image, "freq")
    returned = lax.all_to_all(
        residual.reshape(2, facet_count, capacity), "facet", split_axis=1, concat_axis=1, tiled=True
    )
    returned = returned.reshape(2, facet_count * capacity)
    return (current, returned[:, slot_index])


def solution(mesh):
    return jax.shard_map(
        on_device,
        mesh=mesh,
        in_specs=(
            P("facet", None),
            P(None, ("freq", "facet")),
            P(None, ("freq", "facet")),
            P(None, ("freq", "facet")),
            P(("freq", "facet"), None),
            P(None, ("freq", "facet")),
            P("freq", None, None),
        ),
        out_specs=(P("facet", None), P(None, ("freq", "facet"))),
        check_vma=False,
    )
```

profile of v0, /device:TPU:0, one launch (start us, length us, event | category | flops | bytes accessed | tf_op | source)
XLA Modules:
  0.0 240.4 jit_solution(4313704084468116243)
XLA Ops:
  7.2 0.7 fusion.247
  7.8 0.6 reduce-window.6
  8.6 0.8 fusion.246
  9.4 0.7 compare_select_fusion.6
  10.1 0.7 convert_element_type.365
  10.8 0.7 maximum_bitcast_fusion
  11.6 1.3 scatter_custom_fusion
  13.2 0.9 reshape.2303
  14.1 7.4 %all-to-all-start = ((f32[16,1,2304]{2,1,0:T(1,128)}), f32[16,1,2304]{2,1,0:T(1,128)S(1)}, u32[]{:S(2)}, u32[]{:S(2)}) async-start(f32[16,1,2304]{2,1,0:T(1,128)} %reshape.2303), calls=%async_computation | async-start | bytes 294912 | tf_op jit(solution)/shard_map/all_to_all | solution.py:187
  21.5 0.7 all-gather.3.cloned.1.call-update
  22.3 2.2 negate_convert_fusion
  24.4 2.0 fusion.234
  26.6 0.5 fusion.252
  27.1 4.4 %sine_convert_fusion = (bf16[2048,64]{1,0:T(8,128)(2,1)S(1)}, bf16[2048,64]{1,0:T(8,128)(2,1)S(1)}) fusion(), kind=kLoop, calls=%fused_computation.325 | loop fusion | flops 2097152 | bytes 524288 | tf_op jit(solution)/shard_map/convert.11
  31.9 0.6 broadcast.2851
  32.5 1.0 reduce.138
  37.0 0.5 select_add_fusion.2
  37.5 0.5 select_add_fusion.3
  38.1 25.6 %all-gather.3.cloned.1.call-done = f32[128,2048]{1,0:T(8,128)} async-done(((f32[8,2048]{1,0:T(8,128)}), f32[128,2048]{1,0:T(8,128)}) %all-gather.3.cloned.1.call-update) | async-done | bytes 1048592 | tf_op jit(solution)/shard_map/all_gather | solution.py:202
  63.7 11.2 %while.58 = (s32[]{:T(128)}, f32[64,2,64]{2,0,1:T(8,128)S(1)}, s32[]{:T(128)}, s32[2,8]{1,0:T(2,128)S(1)}, f32[2,8,8,2048]{3,2,1,0:T(8,128)}, /*index=5*/s32[]{:...) while((s32[]{:T(128)}, f32[64,2,64]{2,0,1:T(8,128)S(1)}, s32[]{:T(128)}, ...), condition=%wide.region_5.6_spmd.clone, body=%wide.region_4.5_spmd.clone.sunk | while | flops 80678272 | bytes 6762359 | solution.py:82
  63.7 0.8 fusion.335
  64.5 1.3 fusion.336
  66.1 1.2 iota_add_fusion.18
  69.4 0.8 fusion.335
  70.1 1.3 fusion.336
  71.7 1.2 iota_add_fusion.18
  75.0 0.6 fusion.210
  75.6 0.9 fusion.225
  76.4 22.5 %all_gather.13 = f32[1024,2,64]{2,0,1:T(8,128)S(1)} all-gather(f32[64,2,64]{2,0,1:T(8,128)S(1)} %fusion.225), channel_id=1, replica_groups=mesh['freq'=2,'facet'=16] {'facet'}, dimensions={0}, use_global_device_ids=true | all-gather | bytes 557056 | tf_op jit(solution)/shard_map/all_gather | solution.py:215
  98.9 6.5 %while.59 = (s32[]{:T(128)}, f32[8,2048]{1,0:T(8,128)S(1)}, s32[2,8,2]{1,2,0:T(2,128)S(1)}, s32[]{:T(128)}, f32[2,8,64,2,64]{4,2,1,0,3:T(8,128)S(1)}, /*index=5*...) while((s32[]{:T(128)}, f32[8,2048]{1,0:T(8,128)S(1)}, s32[2,8,2]{1,2,0:T(2,128)S(1)}, ...), condition=%wide.region_9.10_spmd.clone, body=%wide.region_7.9_spmd.clone.sunk | while | flops 80773128 | bytes 5456375 | solution.py:135
  99.6 0.5 convolution_subtract_fusion.4
  100.1 0.5 fusion.347
  100.8 0.5 subtract_convert_fusion.4
  102.8 0.5 convolution_subtract_fusion.4
  104.0 0.5 subtract_convert_fusion.4
  105.4 0.6 broadcast_multiply_fusion.1
  106.1 18.3 %all-reduce.3.cloned.1.call-done = f32[8,2048]{1,0:T(8,128)} async-done(((f32[8,2048]{1,0:T(8,128)}), f32[8,2048]{1,0:T(8,128)}) %all-reduce.3.cloned.1.call-update) | async-done | bytes 65552 | tf_op jit(solution)/shard_map/psum | solution.py:220
  124.4 1.5 multiply_add_fusion.5
  125.9 39.1 %all-gather.5.cloned.1.call-done = f32[128,2048]{1,0:T(8,128)} async-done(((f32[8,2048]{1,0:T(8,128)}), f32[128,2048]{1,0:T(8,128)}) %all-gather.5.cloned.1.call-update) | async-done | bytes 1048592 | tf_op jit(solution)/shard_map/all_gather | solution.py:202
  165.0 11.2 %while.60 = (s32[]{:T(128)}, f32[64,2,64]{2,0,1:T(8,128)S(1)}, s32[]{:T(128)}, s32[2,8]{1,0:T(2,128)S(1)}, f32[2,8,8,2048]{3,2,1,0:T(8,128)}, /*index=5*/s32[]{:...) while((s32[]{:T(128)}, f32[64,2,64]{2,0,1:T(8,128)S(1)}, s32[]{:T(128)}, ...), condition=%wide.region_12.13_spmd.clone, body=%wide.region_11.12_spmd.clone.sunk | while | flops 80678272 | bytes 6762359 | solution.py:82
  165.0 0.8 fusion.365
  165.8 1.3 fusion.366
  167.4 1.2 iota_add_fusion.22
  170.7 0.8 fusion.365
  171.4 1.3 fusion.366
  173.0 1.2 iota_add_fusion.22
  176.3 0.6 fusion.211
  177.0 0.7 reshape.2305
  177.7 3.7 %all-to-all-start.1 = ((f32[16,1,128]{2,1,0:T(1,128)}), f32[16,1,128]{2,1,0:T(1,128)S(1)}, u32[]{:S(2)}, u32[]{:S(2)}) async-start(f32[16,1,128]{2,1,0:T(1,128)} %reshape.2305), calls=%async_computation.1 | async-start | bytes 16384 | tf_op jit(solution)/shard_map/all_to_all | solution.py:221
  181.4 0.9 fusion.221
  182.3 24.6 %all_gather.15 = f32[1024,2,64]{2,0,1:T(8,128)S(1)} all-gather(f32[64,2,64]{2,0,1:T(8,128)S(1)} %fusion.221), channel_id=1, replica_groups=mesh['freq'=2,'facet'=16] {'facet'}, dimensions={0}, use_global_device_ids=true | all-gather | bytes 557056 | tf_op jit(solution)/shard_map/all_gather | solution.py:215
  206.9 6.5 %while.61 = (s32[]{:T(128)}, f32[8,2048]{1,0:T(8,128)S(1)}, s32[2,8,2]{1,2,0:T(2,128)S(1)}, s32[]{:T(128)}, f32[2,8,64,2,64]{4,2,1,0,3:T(8,128)S(1)}, /*index=5*...) while((s32[]{:T(128)}, f32[8,2048]{1,0:T(8,128)S(1)}, ...), condition=%wide.region_16.17_spmd.clone, body=%wide.region_14.16_spmd.clone.sunk | while | flops 80773128 | bytes 5456375 | solution.py:135
  207.6 0.5 convolution_subtract_fusion.5
  208.1 0.5 fusion.377
  208.8 0.5 subtract_convert_fusion.5
  210.8 0.5 convolution_subtract_fusion.5
  211.3 0.5 fusion.377
  212.0 0.5 subtract_convert_fusion.5
  213.4 0.6 broadcast_multiply_fusion
  214.1 0.7 reduce.139
  215.1 0.7 gather_fusion
  215.8 0.7 copy.46
  216.5 15.9 %all-reduce.5.cloned.1.call-done = f32[8,2048]{1,0:T(8,128)} async-done(((f32[8,2048]{1,0:T(8,128)}), f32[8,2048]{1,0:T(8,128)}) %all-reduce.5.cloned.1.call-update) | async-done | bytes 65552 | tf_op jit(solution)/shard_map/psum | solution.py:220
  232.4 1.5 multiply_add_fusion.4
  (178 shorter events, 21.1 us)
Async XLA Ops:
  12.9 13.5 %copy-start.4 = (s32[1,16,2]{1,2,0:T(2,128)S(1)}, s32[1,16,2]{1,2,0:T(2,128)}, u32[]{:S(2)}) copy-start(s32[1,16,2]{1,2,0:T(2,128)} %param.21) | copy-start | bytes 388
  14.1 17.9 %all-to-all-start = ((f32[16,1,2304]{2,1,0:T(1,128)}), f32[16,1,2304]{2,1,0:T(1,128)S(1)}, u32[]{:S(2)}, u32[]{:S(2)}) async-start(f32[16,1,2304]{2,1,0:T(1,128)} %reshape.2303), calls=%async_computation | async-start | bytes 294912 | tf_op jit(solution)/shard_map/all_to_all | solution.py:187
  21.5 42.2 %all-gather.3.cloned.1.call-start = ((), (), s32[]{:S(2)}) async-start(), calls=%async_computation.2 | async-start | bytes 1114112 | tf_op jit(solution)/shard_map/all_gather | solution.py:202
  22.2 102.2 %all-reduce.3.cloned.1.call-start = ((), (), s32[]{:S(2)}) async-start(), calls=%async_computation.3 | async-start | bytes 131072 | tf_op jit(solution)/shard_map/psum | solution.py:220
  63.7 2.1 copy-start
  69.3 2.1 copy-start
  98.9 25.5 %copy-start.3 = (f32[8,2048]{1,0:T(8,128)S(1)}, f32[8,2048]{1,0:T(8,128)}, u32[]{:S(2)}) copy-start(f32[8,2048]{1,0:T(8,128)} %param.15) | copy-start | bytes 196612
  106.1 59.0 %all-gather.5.cloned.1.call-start = ((), (), s32[]{:S(2)}) async-start(), calls=%async_computation.4 | async-start | bytes 1114112 | tf_op jit(solution)/shard_map/all_gather | solution.py:202
  165.0 2.1 copy-start.1
  170.6 2.1 copy-start.1
  177.7 36.4 %all-to-all-start.1 = ((f32[16,1,128]{2,1,0:T(1,128)}), f32[16,1,128]{2,1,0:T(1,128)S(1)}, u32[]{:S(2)}, u32[]{:S(2)}) async-start(f32[16,1,128]{2,1,0:T(1,128)} %reshape.2305), calls=%async_computation.1 | async-start | bytes 16384 | tf_op jit(solution)/shard_map/all_to_all | solution.py:221
  181.3 51.0 %all-reduce.5.cloned.1.call-start = ((), (), s32[]{:S(2)}) async-start(), calls=%async_computation.5 | async-start | bytes 131072 | tf_op jit(solution)/shard_map/psum | solution.py:220
  206.9 25.5 %copy-start.2 = (f32[8,2048]{1,0:T(8,128)S(1)}, f32[8,2048]{1,0:T(8,128)}, u32[]{:S(2)}) copy-start(f32[8,2048]{1,0:T(8,128)} %multiply_add_fusion.5) | copy-start | bytes 196612
Sparse Core Ops, SparseCore 0:
  24.4 39.2 all-gather.2
  106.2 18.1 all-reduce.2
  127.1 37.8 all-gather.4
  214.2 18.1 all-reduce.4
where the time goes:
time: 241 us; the launch traced here: 240 us
  waiting for transfers between devices  99.6 us (41%)
  blocking collectives  47.1 us (20%)
  other arithmetic  32.1 us (13%)
  matrix products  25.6 us (11%)
  between operations  14.1 us (6%)
  starting transfers between devices  11.3 us (5%)
  local copies, waits for them, and re-layouts  10 us (4%)
    all_gather x2, waiting for transfers between devices, on_device(): gathered = lax.all_gather(current, 'facet', axis=0, tiled=True)  64.7 us
    all_gather x2, blocking collectives, on_device(): add_gathered = lax.all_gather(gridded, 'facet', axis=0, tiled=True)  47.1 us
    psum x2, waiting for transfers between devices, on_device(): current = current + GAIN_STEP * lax.psum(dirty_image, 'freq')  34.2 us
    another operation x5, other arithmetic  9.08 us
    all_to_all x1, starting transfers between devices, on_device(): lax.all_to_all(send_buffer, 'facet', split_axis=1, concat_axis=1, tiled=T...  7.41 us
    dot_general x4, matrix products, forward_part(): jnp.dot(imag_mod, table_half, preferred_element_type=jnp.float32)  5.08 us
  transfers between devices with their start and end apart: 6, of which 4 were waited for; matrix products, arithmetic and copies ran while one was open for 11% of the time, Pallas kernels for 0%

commit v1 on v0

v1 whole, which is shorter than its diff:
```python
import math

import jax
import jax.numpy as jnp
from jax import lax
from jax.experimental import pallas as pl
from jax.experimental.pallas import tpu as pltpu
from jax.sharding import PartitionSpec as P

GRID = 16384
FACET = 2048
FROWS = 8
SUB = 64
SUPPORT = 16
LANES = 128
ACROSS = GRID // FACET
GROUPS = 5
GAIN_STEP = 0.5

F32 = jnp.float32
BF16 = jnp.bfloat16
I32 = jnp.int32
exact_products = lax.Precision.HIGHEST


def iota(shape, dim):
    return lax.broadcasted_iota(I32, shape, dim)


def phase_pair(index):
    moved = index + GRID // 8
    quadrant = (moved >> 12) & 3
    angle = ((moved & (GRID // 4 - 1)) - GRID // 8).astype(F32) * (2.0 * math.pi / GRID)
    sq = angle * angle
    sin_p = angle * (1.0 + sq * (-1.0 / 6 + sq * (1.0 / 120 + sq * (-1.0 / 5040 + sq * (1.0 / 362880)))))
    cos_p = 1.0 + sq * (-0.5 + sq * (1.0 / 24 + sq * (-1.0 / 720 + sq * (1.0 / 40320))))
    swap = (quadrant & 1) == 1
    cos_v = jnp.where(swap, sin_p, cos_p)
    sin_v = jnp.where(swap, cos_p, sin_p)
    cos_v = jnp.where((quadrant == 1) | (quadrant == 2), -cos_v, cos_v)
    sin_v = jnp.where(quadrant >= 2, -sin_v, sin_v)
    return cos_v, sin_v


def phase_rows(freq):
    cos_v, sin_v = phase_pair(freq * iota(freq.shape, 1))
    turn_c, turn_s = phase_pair(freq * LANES)
    cos_l, sin_l = [cos_v], [sin_v]
    while len(cos_l) < FACET // LANES:
        more_c = [c * turn_c - s * turn_s for c, s in zip(cos_l, sin_l)]
        more_s = [s * turn_c + c * turn_s for c, s in zip(cos_l, sin_l)]
        cos_l, sin_l = cos_l + more_c, sin_l + more_s
        turn_c, turn_s = turn_c * turn_c - turn_s * turn_s, 2.0 * turn_c * turn_s
    return jnp.concatenate(cos_l, axis=1), jnp.concatenate(sin_l, axis=1)


def dot_nt(left, right, precision=None):
    return lax.dot_general(
        left, right, (((1,), (1,)), ((), ())), precision=precision, preferred_element_type=F32
    )


def dot_nn(left, right, precision=None):
    return lax.dot_general(
        left, right, (((1,), (0,)), ((), ())), precision=precision, preferred_element_type=F32
    )


def layout_of(cap):
    lane_groups = LANES // cap
    row_blocks = -(-GROUPS // lane_groups)
    return lane_groups, row_blocks, FROWS + 8 * row_blocks


def slot_parts(owner_row, count):
    rows = owner_row.shape[1]
    hits = (iota((count, rows), 0) == owner_row).astype(F32)
    earlier = (iota((rows, rows), 0) < iota((rows, rows), 1)).astype(F32)
    before = dot_nn(hits.astype(BF16), earlier.astype(BF16))
    return hits, jnp.sum(before * hits, axis=0, keepdims=True).astype(I32)


def splat_rows(corner_ref, target_ref, start, count, step):
    for s in range(count):
        target_ref[pl.ds(start + s, 1), :] = jnp.full((1, LANES), corner_ref[step * s], I32)


def send_kernel(
    corner_ref, owner_ref, vis_ref, ku_ref, kv_ref, off_ref, image_ref,
    send_ref, table_ref, freq_ref, mod_ref, *, count, cap,
):
    lane_groups, row_blocks, piece = layout_of(cap)
    facet = lax.axis_index("facet")
    x_start = facet % ACROSS * FACET - GRID // 2
    splat_rows(corner_ref, freq_ref, 0, count, 2)
    freq = freq_ref[...]
    cos_t, sin_t = phase_rows(iota((SUB, LANES), 0))
    table = jnp.concatenate([cos_t, sin_t], axis=0).astype(BF16)
    table_ref[...] = table
    cos_u, sin_u = phase_rows(freq)
    image = image_ref[...]
    for s in range(count):
        both = jnp.concatenate([image * cos_u[s : s + 1], -image * sin_u[s : s + 1]], axis=0)
        mod_ref[16 * s : 16 * s + 16, :] = both.astype(BF16)
    prod = dot_nt(mod_ref[...], table)
    lane = iota((FROWS, LANES), 1)
    low = lane < SUB
    cos_x, sin_x = phase_pair((freq + (iota(freq.shape, 1) & (SUB - 1))) * x_start)
    sin_x = jnp.where(iota(freq.shape, 1) < SUB, sin_x, -sin_x)
    for s in range(count):
        real_p = prod[16 * s : 16 * s + 8]
        imag_p = pltpu.roll(prod[16 * s + 8 : 16 * s + 16], SUB, 1)
        col = jnp.where(low, real_p + imag_p, imag_p - real_p)
        send_ref[piece * s : piece * s + FROWS, :] = (
            col * cos_x[s : s + 1] + pltpu.roll(col, SUB, 1) * sin_x[s : s + 1]
        )

    owner_row = owner_ref[...]
    rows = owner_row.shape[1]
    hits, rank = slot_parts(owner_row, count)
    blank = jnp.zeros((4, rows), F32)
    misc = jnp.concatenate([vis_ref[...], off_ref[...].astype(F32), blank], axis=0)
    parts = [ku_ref[0:8, :], ku_ref[8:16, :], kv_ref[0:8, :], kv_ref[8:16, :], misc]
    total = jnp.zeros((count * row_blocks * 8, LANES), F32)
    for group in range(lane_groups):
        mine = parts[group * row_blocks : (group + 1) * row_blocks]
        if not mine:
            continue
        if len(mine) < row_blocks:
            mine = mine + [jnp.zeros((8, rows), F32)] * (row_blocks - len(mine))
        stacked = jnp.concatenate(mine, axis=0)
        masked = jnp.concatenate([stacked * hits[s : s + 1] for s in range(count)], axis=0)
        place = (iota((LANES, rows), 0) == rank + group * cap).astype(F32)
        total = total + dot_nt(masked, place, exact_products)
    for s in range(count):
        send_ref[piece * s + FROWS : piece * (s + 1), :] = total[
            8 * row_blocks * s : 8 * row_blocks * (s + 1)
        ]


def place_kernel(taps, offset):
    low = jnp.concatenate([taps, jnp.zeros((8, LANES), F32)], axis=0)
    for step in (1, 2, 4):
        bit = jnp.broadcast_to((offset & step) != 0, low.shape)
        low = jnp.where(bit, pltpu.roll(low, step, 0), low)
    zero = jnp.zeros((8, LANES), F32)
    blocks = [low[0:8], low[8:16], low[16:24]]
    for step in (1, 2, 4):
        bit = jnp.broadcast_to((offset & (8 * step)) != 0, (8, LANES))
        size = min(len(blocks) + step, SUB // 8)
        wide = blocks + [zero] * (size - len(blocks))
        blocks = [jnp.where(bit, wide[k - step] if k >= step else zero, wide[k]) for k in range(size)]
    return jnp.concatenate(blocks, axis=0)


def predict(column_rows, kern_u, kern_h, vis, scale):
    height = column_rows.shape[0]
    stacked = jnp.concatenate([column_rows[:, :SUB], column_rows[:, SUB:]], axis=0)
    partial = dot_nn(stacked, kern_u, exact_products)
    part_re, part_im = partial[:height], partial[height:]
    h_re, h_im = kern_h[:height], kern_h[height:]
    pred_re = jnp.sum(h_re * part_re - h_im * part_im, axis=0, keepdims=True)
    pred_im = jnp.sum(h_re * part_im + h_im * part_re, axis=0, keepdims=True)
    return vis[0:1] - scale * pred_re, vis[1:2] - scale * pred_im


def grid_rows(res_re, res_im, kern_u, kern_h):
    height = kern_h.shape[0] // 2
    h_re, h_im = kern_h[:height], kern_h[height:]
    spread = jnp.concatenate([h_re * res_re + h_im * res_im, h_re * res_im - h_im * res_re], axis=0)
    rows = dot_nt(spread, kern_u, exact_products)
    return jnp.concatenate([rows[:height], rows[height:]], axis=1)


def first_kernel(
    corner_ref, got_ref, col_ref, ku_ref, kh_ref, vis_ref, rows_ref, own_ref, *, count, cap, groups, scale,
):
    lane_groups, row_blocks, piece = layout_of(cap)
    height = count // ACROSS * FROWS
    v_start = corner_ref[2 * lax.axis_index("facet") + 1]
    sums = []
    for down in range(count // ACROSS):
        total = got_ref[piece * down * ACROSS : piece * down * ACROSS + FROWS, :]
        for across in range(1, ACROSS):
            at = piece * (down * ACROSS + across)
            total = total + got_ref[at : at + FROWS, :]
        sums.append(total)
    columns = jnp.concatenate(sums, axis=0)
    col_ref[...] = columns
    lane_group = iota((8, LANES), 1) // cap
    u_list, v_list, vis_list = [], [], []
    for tile in range(count // lane_groups):
        found = []
        for k in range(GROUPS):
            block, group = k % row_blocks, k // row_blocks
            value = None
            for j in range(lane_groups):
                at = piece * (tile * lane_groups + j) + FROWS + 8 * block
                moved = got_ref[at : at + 8, :]
                shift = (j - group) * cap % LANES
                if shift:
                    moved = pltpu.roll(moved, shift, 1)
                value = moved if value is None else jnp.where(lane_group == j, moved, value)
            found.append(value)
        misc = found[4]
        u_list.append(place_kernel(jnp.concatenate(found[0:2], axis=0), misc[2:3].astype(I32)))
        v_list.append(place_kernel(jnp.concatenate(found[2:4], axis=0), misc[3:4].astype(I32)))
        vis_list.append(misc)
    kern_u = jnp.concatenate(u_list, axis=1)
    kern_v = jnp.concatenate(v_list, axis=1)
    vis = jnp.concatenate(vis_list, axis=1)
    row = iota((height, SUB), 0)
    y_pos = row // FROWS * FACET - GRID // 2 + row % FROWS
    cos_y, sin_y = phase_pair((v_start + iota((height, SUB), 1)) * y_pos)
    kern_h = dot_nn(jnp.concatenate([cos_y, -sin_y], axis=0), kern_v, exact_products)
    ku_ref[...] = kern_u
    kh_ref[...] = kern_h
    vis_ref[...] = vis
    res_re, res_im = predict(columns, kern_u, kern_h, vis, scale)
    rows = grid_rows(res_re, res_im, kern_u, kern_h)
    own_ref[...] = rows
    for d in range(groups * count):
        rows_ref[height * d : height * (d + 1), :] = rows


def group_corner(corner_ref, near_refs, group, groups, index):
    refs = [corner_ref] + list(near_refs)
    back = (lax.axis_index("freq") - group) % groups
    value = refs[0][2 * index]
    for k in range(1, groups):
        value = jnp.where(back == k, refs[k][2 * index], value)
    return value


def second_kernel(*refs, count, cap, groups, scale):
    corner_ref, near_refs = refs[0], refs[1:groups]
    all_ref, own_ref, col_ref, ku_ref, kh_ref, vis_ref, back_ref, sum_ref = refs[groups:]
    lane_groups = LANES // cap
    height = col_ref.shape[0]
    u_start = corner_ref[2 * lax.axis_index("facet")]
    sum_ref[...] = jnp.zeros_like(sum_ref)
    row, col = iota((LANES, LANES), 0), iota((LANES, LANES), 1)
    same = (row < SUB) == (col < SUB)
    row_a, col_a = row & (SUB - 1), col & (SUB - 1)
    sign = jnp.where(col < SUB, 1.0, -1.0)
    half = GRID // 2

    def overlap(d, carry):
        u_other = group_corner(corner_ref, near_refs, d // count, groups, d % count)
        ahead = ((u_start - u_other + half) & (GRID - 1)) - half
        mirror = (-u_start - u_other) & (GRID - 1)

        @pl.when(((ahead > -SUB) & (ahead < SUB)) | (mirror < 2 * SUB - 1))
        def _():
            select = jnp.where(same & (row_a == col_a + ahead), 1.0, 0.0)
            select = select + jnp.where(same & (row_a + col_a == mirror), sign, 0.0)
            block = all_ref[pl.ds(pl.multiple_of(d * height, 8), height), :]
            sum_ref[...] += dot_nn(block, select, exact_products)

        return carry

    lax.fori_loop(0, groups * count, overlap, 0)
    columns = col_ref[...] + (GAIN_STEP * scale * (GRID / 2)) * sum_ref[...]
    kern_u, kern_h = ku_ref[...], kh_ref[...]
    res_re, res_im = predict(columns, kern_u, kern_h, vis_ref[...], scale)
    rows = own_ref[...] + grid_rows(res_re, res_im, kern_u, kern_h)
    res = jnp.concatenate([res_re, res_im, jnp.zeros((6, res_re.shape[1]), F32)], axis=0)
    for s in range(count):
        tile, j = s // lane_groups, s % lane_groups
        block = res[:, LANES * tile : LANES * (tile + 1)]
        if j:
            block = pltpu.roll(block, LANES - j * cap, 1)
        down = s // ACROSS
        for g in range(groups):
            at = 16 * (g * count + s)
            back_ref[at : at + 8, :] = rows[8 * down : 8 * down + 8]
            back_ref[at + 8 : at + 16, :] = block


def image_kernel(*refs, count, groups, scale):
    corner_ref, near_refs = refs[0], refs[1:groups]
    got_ref, table_ref, owner_ref, image_ref, out_ref, res_ref, freq_ref = refs[groups:]
    total = groups * count
    facet = lax.axis_index("facet")
    x_start = facet % ACROSS * FACET - GRID // 2
    for g in range(groups):
        for s in range(count):
            d = g * count + s
            u_other = group_corner(corner_ref, near_refs, g, groups, s)
            freq_ref[d : d + 1, :] = jnp.full((1, LANES), u_other, I32)
    freq = freq_ref[...]
    low = iota((FROWS, LANES), 1) < SUB
    cos_x, sin_x = phase_pair((freq + (iota(freq.shape, 1) & (SUB - 1))) * x_start)
    sin_x = jnp.where(iota(freq.shape, 1) < SUB, -sin_x, sin_x)
    left = []
    for d in range(total):
        block = got_ref[16 * d : 16 * d + 8, :]
        moved = block * cos_x[d : d + 1] + pltpu.roll(block, SUB, 1) * sin_x[d : d + 1]
        left.append(jnp.where(low, moved, -moved))
        left.append(pltpu.roll(moved, SUB, 1))
    left = jnp.concatenate(left, axis=0).astype(BF16)
    cos_u, sin_u = phase_rows(freq)
    both = dot_nn(left, table_ref[...])
    dirty = jnp.zeros((FROWS, FACET), F32)
    for d in range(total):
        dirty = dirty + both[16 * d : 16 * d + 8] * cos_u[d : d + 1]
        dirty = dirty - both[16 * d + 8 : 16 * d + 16] * sin_u[d : d + 1]
    out_ref[...] = image_ref[...] + (GAIN_STEP * scale) * dirty

    owner_row = owner_ref[...]
    rows = owner_row.shape[1]
    hits, rank = slot_parts(owner_row, count)
    first = lax.axis_index("freq") * (count * 16)
    back = [got_ref[pl.ds(pl.multiple_of(first + 16 * s + 8, 8), 8), :] for s in range(count)]
    place = (iota((LANES, rows), 0) == rank).astype(F32)
    found = dot_nn(jnp.concatenate(back, axis=0), place, exact_products)
    picked = jnp.zeros((8, rows), F32)
    for s in range(count):
        picked = picked + found[8 * s : 8 * s + 8] * hits[s : s + 1]
    res_ref[...] = picked[0:2]


def on_device(model_image, visibilities, kernel_u, kernel_v, owners, offsets, corners):
    count = lax.axis_size("facet")
    groups = lax.axis_size("freq")
    rows = owners.shape[0]
    cap = 4 * rows // count
    assert count % ACROSS == 0 and LANES % cap == 0
    scale = 1.0 / math.sqrt(count * FROWS * FACET)
    lane_groups, row_blocks, piece = layout_of(cap)
    height = count // ACROSS * FROWS
    slots = count * cap
    total = groups * count
    corner = corners.reshape(2 * count)
    near = [
        lax.ppermute(corner, "freq", [(g, (g + k) % groups) for g in range(groups)])
        for k in range(1, groups)
    ]
    owner_row = owners.reshape(1, rows)
    smem = pl.BlockSpec(memory_space=pltpu.SMEM)
    vmem = pl.BlockSpec(memory_space=pltpu.VMEM)
    params = pltpu.CompilerParams(vmem_limit_bytes=48 * 1024 * 1024)

    def shape(*dims, dtype=F32):
        return jax.ShapeDtypeStruct(dims, dtype)

    def call(body, out_shape, scalars, arrays, name, scratch=(), **sizes):
        return pl.pallas_call(
            lambda *refs: body(*refs, **sizes),
            out_shape=out_shape,
            in_specs=[smem] * len(scalars) + [vmem] * len(arrays),
            out_specs=jax.tree.map(lambda _: vmem, out_shape),
            scratch_shapes=scratch,
            compiler_params=params,
            name=name,
        )(*scalars, *arrays)

    send, table = call(
        send_kernel,
        (shape(count * piece, LANES), shape(2 * SUB, FACET, dtype=BF16)),
        [corner],
        [owner_row, visibilities, kernel_u, kernel_v, offsets, model_image],
        "send_rows",
        [pltpu.VMEM((count, LANES), I32), pltpu.VMEM((16 * count, FACET), BF16)],
        count=count,
        cap=cap,
    )
    got = lax.all_to_all(send, "facet", split_axis=0, concat_axis=0, tiled=True)
    columns, kern_u, kern_h, vis, spread, own = call(
        first_kernel,
        (
            shape(height, LANES),
            shape(SUB, slots),
            shape(2 * height, slots),
            shape(8, slots),
            shape(total * height, LANES),
            shape(height, LANES),
        ),
        [corner],
        [got],
        "first_cycle",
        count=count,
        cap=cap,
        groups=groups,
        scale=scale,
    )
    everyone = lax.all_to_all(spread, ("freq", "facet"), split_axis=0, concat_axis=0, tiled=True)
    back = call(
        second_kernel,
        shape(total * 16, LANES),
        [corner, *near],
        [everyone, own, columns, kern_u, kern_h, vis],
        "second_cycle",
        [pltpu.VMEM((height, LANES), F32)],
        count=count,
        cap=cap,
        groups=groups,
        scale=scale,
    )
    returned = lax.all_to_all(back, ("freq", "facet"), split_axis=0, concat_axis=0, tiled=True)
    return call(
        image_kernel,
        (shape(FROWS, FACET), shape(2, rows)),
        [corner, *near],
        [returned, table, owner_row, model_image],
        "form_image",
        [pltpu.VMEM((total, LANES), I32)],
        count=count,
        groups=groups,
        scale=scale,
    )


def solution(mesh):
    return jax.shard_map(
        on_device,
        mesh=mesh,
        in_specs=(
            P("facet", None),
            P(None, ("freq", "facet")),
            P(None, ("freq", "facet")),
            P(None, ("freq", "facet")),
            P(("freq", "facet"), None),
            P(None, ("freq", "facet")),
            P("freq", None, None),
        ),
        out_specs=(P("facet", None), P(None, ("freq", "facet"))),
        check_vma=False,
    )
```

time: 241 us -> 56.7 us (0.24)
  waiting for transfers between devices: 99.6 us -> 8.42 us
  other arithmetic: 32.1 us -> 0 us
  matrix products: 25.6 us -> 0 us
  blocking collectives: 47.1 us -> 30.1 us
  between operations: 14.1 us -> 0.7 us
  Pallas kernels: 0 us -> 8.77 us
  starting transfers between devices: 11.3 us -> 4.62 us
  local copies, waits for them, and re-layouts: 10 us -> 3.76 us
    all_gather x2 -> x0, waiting for transfers between devices: 64.7 us -> none  [on_device(): gathered = lax.all_gather(current, 'facet', axis=0, tiled=True)]
    all_gather x2 -> x0, blocking collectives: 47.1 us -> none  [on_device(): add_gathered = lax.all_gather(gridded, 'facet', axis=0, tiled=True)]
    psum x2 -> x0, waiting for transfers between devices: 34.2 us -> none  [on_device(): current = current + GAIN_STEP * lax.psum(dirty_image, 'freq')]
    all_to_all x0 -> x2, blocking collectives: none -> 30.1 us  [the longest x1 17.2 us: on_device(): got = lax.all_to_all(send, 'facet', split_axis=0, concat_axis=0, tiled=True)]
    dot_general x48 -> x0, matrix products: 25.6 us -> none  [the longest x4 5.08 us: forward_part(): jnp.dot(imag_mod, table_half, preferred_element_type=jnp.float32)]
    add x30 -> x0, other arithmetic: 9.57 us -> none  [the longest x4 4.8 us: forward_part(): cos_x, sin_x = phase_pair(u_start + frequency[None, :], x_start[:, None])]
    another operation x5 -> x0, other arithmetic: 9.08 us -> none
    pallas_call x0 -> x4, Pallas kernels: none -> 8.77 us  [call(): pl.pallas_call(lambda *refs: body(*refs, **sizes), out_shape=out_shape, i...]
  transfers between devices with their start and end apart: 6 -> 2, of which waited for: 4 -> 2; matrix products, arithmetic and copies ran while one was open for 11% -> 0% of each run, Pallas kernels for 0% -> 0%
where the time goes in v1:
time: 56.7 us; the launch traced here: 56.4 us
  blocking collectives  30.1 us (53%)
  Pallas kernels  8.77 us (15%)
  waiting for transfers between devices  8.42 us (15%)
  starting transfers between devices  4.62 us (8%)
  local copies, waits for them, and re-layouts  3.76 us (7%)
  between operations  0.7 us (1%)
    all_to_all x1, blocking collectives, on_device(): got = lax.all_to_all(send, 'facet', split_axis=0, concat_axis=0, tiled=True)  17.2 us
    all_to_all x1, blocking collectives, on_device(): lax.all_to_all(back, ('freq', 'facet'), split_axis=0, concat_axis=0, tile...  12.9 us
    pallas_call x4, Pallas kernels, call(): pl.pallas_call(lambda *refs: body(*refs, **sizes), out_shape=out_shape, i...  8.77 us
    all_to_all x1, waiting for transfers between devices, on_device(): lax.all_to_all(spread, ('freq', 'facet'), split_axis=0, concat_axis=0, ti...  6.41 us
    unnamed x15, local copies, waits for them, and re-layouts  3.68 us
    all_to_all x1, starting transfers between devices, on_device(): lax.all_to_all(spread, ('freq', 'facet'), split_axis=0, concat_axis=0, ti...  2.79 us
    ppermute x1, waiting for transfers between devices, on_device(): lax.ppermute(corner, 'freq', [(g, (g + k) % groups) for g in range(groups)])  2.01 us
    ppermute x1, starting transfers between devices, on_device(): lax.ppermute(corner, 'freq', [(g, (g + k) % groups) for g in range(groups)])  1.83 us
  transfers between devices with their start and end apart: 2, of which 2 were waited for; matrix products, arithmetic and copies ran while one was open for 0% of the time, Pallas kernels for 0%

profile of v1, /device:TPU:0, one launch (start us, length us, event | category | flops | bytes accessed | tf_op | source)
XLA Modules:
  0.0 56.4 jit_solution(17635373358950656699)
XLA Ops:
  0.6 0.0 copy-start.2
  0.6 0.8 %copy.10 = s32[1,16,2]{2,1,0:T(8,128)S(1)} copy(s32[1,16,2]{1,2,0:T(2,128)} %param.13) | data formatting | bytes 256 | tf_op args[6]
  1.4 0.0 copy-start.5
  1.4 0.1 reshape.16.refs_0_
  1.5 0.0 copy-start.4
  1.5 0.0 copy-done.2
  1.5 0.6 %copy-done.5 = f32[2,256]{1,0:T(2,128)S(1)} copy-done((f32[2,256]{1,0:T(2,128)S(1)}, f32[2,256]{1,0:T(2,128)}, u32[]{:S(2)}) %copy-start.5) | copy-done | bytes 2072
  2.1 0.1 copy-done.4
  2.2 0.0 copy-start
  2.2 0.8 %copy-done = f32[8,2048]{1,0:T(8,128)S(1)} copy-done((f32[8,2048]{1,0:T(8,128)S(1)}, f32[8,2048]{1,0:T(8,128)}, u32[]{:S(2)}) %copy-start) | copy-done | bytes 65560
  3.0 0.0 copy-start.3
  3.0 0.7 %copy-done.3 = f32[16,256]{1,0:T(8,128)S(1)} copy-done((f32[16,256]{1,0:T(8,128)S(1)}, f32[16,256]{1,0:T(8,128)}, u32[]{:S(2)}) %copy-start.3) | copy-done | bytes 16408
  3.7 0.0 copy-start.6
  3.7 0.7 %copy-done.6 = s32[2,256]{1,0:T(2,128)S(1)} copy-done((s32[2,256]{1,0:T(2,128)S(1)}, s32[2,256]{1,0:T(2,128)}, u32[]{:S(2)}) %copy-start.6) | copy-done | bytes 2072
  4.4 1.8 %send_rows.1 = (f32[512,128]{1,0:T(8,128)S(1)}, bf16[128,2048]{1,0:T(8,128)(2,1)S(1)}) custom-call(s32[32]{0:T(128)S(1)} %reshape.16.refs_0_, s32[1,256]{1,0:T(1,128)S(1)} %bitcast.12, f32[2,256]{1,0:T(2,128)S(1)} %copy-done.5, f32[16,256]{1,0:T(8,128)S(1)} %copy-done.2, f32[16,256]{1,0:T(8,128)S(1)} %copy-done.3, s32[2,256]{1,0:T(2,128)S(1)} %copy-done.6, ...), custom_call_target="tpu_custom_call" | custom-call | tf_op jit(solution)/shard_map/send_rows/pallas_call | solution.py:348
  6.2 17.2 %all_to_all.33 = f32[16,32,128]{2,1,0:T(8,128)S(1)} all-to-all(f32[16,32,128]{2,1,0:T(8,128)S(1)} %bitcast.11), channel_id=1, replica_groups=mesh['freq'=2,'facet'=16] {'facet'}, dimensions={0} | all-to-all | bytes 524288 | tf_op jit(solution)/shard_map/all_to_all | solution.py:368
  23.5 2.2 %first_cycle.1 = (f32[16,128]{1,0:T(8,128)S(1)}, f32[64,1024]{1,0:T(8,128)S(1)}, f32[32,1024]{1,0:T(8,128)S(1)}, f32[8,1024]{1,0:T(8,128)S(1)}, f32[512,128]{1,0:T(8,128)}, /*index=5*/f32[16,128]{1,0:T(8,128)S(1)}) custom-call(s32[32]{0:T(128)S(1)} %reshape.16.refs_0_, f32[512,128]{1,0:T(8,128)S(1)} %bitcast.9), custom_call_target="tpu_custom_call" | custom-call | tf_op jit(solution)/shard_map/first_cycle/pallas_call | solution.py:348
  25.7 2.8 %all-to-all-start.1 = ((f32[32,16,128]{2,1,0:T(8,128)}), f32[32,16,128]{2,1,0:T(8,128)S(1)}, u32[]{:S(2)}, u32[]{:S(2)}) async-start(f32[32,16,128]{2,1,0:T(8,128)} %bitcast.3), calls=%async_computation.1 | async-start | bytes 524288 | tf_op jit(solution)/shard_map/all_to_all | solution.py:387
  28.5 1.8 %collective-permute-start = (s32[32]{0:T(128)S(1)}, s32[32]{0:T(128)S(1)}, u32[]{:S(2)}, u32[]{:S(2)}) collective-permute-start(s32[32]{0:T(128)S(1)} %reshape.16.refs_0_), channel_id=1, source_target_pairs={{0,16},{16,0},{1,17},{17,1},{2,18},{18,2},{3,19},{19,3},{4,20},{20... | collective-permute-start | bytes 392 | tf_op jit(solution)/shard_map/ppermute | solution.py:336
  30.3 2.0 %collective-permute-done.refs_1_ = s32[32]{0:T(128)S(1)} collective-permute-done((s32[32]{0:T(128)S(1)}, s32[32]{0:T(128)S(1)}, u32[]{:S(2)}, u32[]{:S(2)}) %collective-permute-start) | collective-permute-done | bytes 160 | tf_op jit(solution)/shard_map/ppermute | solution.py:336
  32.3 6.4 %all-to-all-done.1 = f32[32,16,128]{2,1,0:T(8,128)S(1)} async-done(((f32[32,16,128]{2,1,0:T(8,128)}), f32[32,16,128]{2,1,0:T(8,128)S(1)}, u32[]{:S(2)}, u32[]{:S(2)}) %all-to-all-start.1) | async-done | bytes 262176 | tf_op jit(solution)/shard_map/all_to_all | solution.py:387
  38.8 2.3 %second_cycle.1 = f32[512,128]{1,0:T(8,128)S(1)} custom-call(s32[32]{0:T(128)S(1)} %reshape.16.refs_0_, s32[32]{0:T(128)S(1)} %collective-permute-done.refs_1_, f32[512,128]{1,0:T(8,128)S(1)} %bitcast.7, f32[16,128]{1,0:T(8,128)S(1)} %get-tuple-element.12.refs_3_, f32[16,128]{1,0:T(8,128)S(1)} %get-tuple-element.13.refs_4_, ...), custom_call_target="tpu_custom_call" | custom-call | tf_op jit(solution)/shard_map/second_cycle/pallas_call | solution.py:348
  41.1 0.0 copy-start.1
  41.1 12.9 %all_to_all.34 = f32[32,16,128]{2,1,0:T(8,128)S(1)} all-to-all(f32[32,16,128]{2,1,0:T(8,128)S(1)} %bitcast.8), channel_id=1, replica_groups=mesh['freq'=2,'facet'=16] {'freq','facet'}, dimensions={0} | all-to-all | bytes 524288 | tf_op jit(solution)/shard_map/all_to_all | solution.py:400
  54.0 0.0 copy-done.1
  54.0 2.4 %form_image.1 = (f32[8,2048]{1,0:T(8,128)}, f32[2,256]{1,0:T(2,128)}) custom-call(s32[32]{0:T(128)S(1)} %reshape.16.refs_0_, s32[32]{0:T(128)S(1)} %collective-permute-done.refs_1_, f32[512,128]{1,0:T(8,128)S(1)} %bitcast.10, bf16[128,2048]{1,0:T(8,128)(2,1)S(1)} %get-tuple-element.17.refs_3_, s32[1,256]{1,0:T(1,128)S(1)} %bitcast.13, f32[8,2048]{1,0:T(8,128)S(1)} %copy-done.1), custom_call_target="tpu_custom_call" | custom-call | tf_op jit(solution)/shard_map/form_image/pallas_call | solution.py:348
Async XLA Ops:
  0.6 0.9 %copy-start.2 = (f32[16,256]{1,0:T(8,128)S(1)}, f32[16,256]{1,0:T(8,128)}, u32[]{:S(2)}) copy-start(f32[16,256]{1,0:T(8,128)} %refs_3_.1) | copy-start | bytes 49156
  1.4 0.7 %copy-start.5 = (f32[2,256]{1,0:T(2,128)S(1)}, f32[2,256]{1,0:T(2,128)}, u32[]{:S(2)}) copy-start(f32[2,256]{1,0:T(2,128)} %refs_2_.1) | copy-start | bytes 6148
  1.5 0.7 %copy-start.4 = (s32[256,1]{0,1:T(1,128)S(1)}, s32[256,1]{0,1:T(1,128)}, u32[]{:S(2)}) copy-start(s32[256,1]{0,1:T(1,128)} %param.11) | copy-start | bytes 3076
  2.2 0.8 %copy-start = (f32[8,2048]{1,0:T(8,128)S(1)}, f32[8,2048]{1,0:T(8,128)}, u32[]{:S(2)}) copy-start(f32[8,2048]{1,0:T(8,128)} %refs_5_.3) | copy-start | bytes 196612
  3.0 0.7 %copy-start.3 = (f32[16,256]{1,0:T(8,128)S(1)}, f32[16,256]{1,0:T(8,128)}, u32[]{:S(2)}) copy-start(f32[16,256]{1,0:T(8,128)} %refs_4_.1) | copy-start | bytes 49156
  3.7 0.7 %copy-start.6 = (s32[2,256]{1,0:T(2,128)S(1)}, s32[2,256]{1,0:T(2,128)}, u32[]{:S(2)}) copy-start(s32[2,256]{1,0:T(2,128)} %refs_5_.2) | copy-start | bytes 6148
  25.7 13.0 %all-to-all-start.1 = ((f32[32,16,128]{2,1,0:T(8,128)}), f32[32,16,128]{2,1,0:T(8,128)S(1)}, u32[]{:S(2)}, u32[]{:S(2)}) async-start(f32[32,16,128]{2,1,0:T(8,128)} %bitcast.3), calls=%async_computation.1 | async-start | bytes 524288 | tf_op jit(solution)/shard_map/all_to_all | solution.py:387
  28.5 3.8 %collective-permute-start = (s32[32]{0:T(128)S(1)}, s32[32]{0:T(128)S(1)}, u32[]{:S(2)}, u32[]{:S(2)}) collective-permute-start(s32[32]{0:T(128)S(1)} %reshape.16.refs_0_), channel_id=1, source_target_pairs={{0,16},{16,0},{1,17},{17,1},{2,18},{18,2},{3,19},{19,3},{4,20},{20... | collective-permute-start | bytes 392 | tf_op jit(solution)/shard_map/ppermute | solution.py:336
  41.1 12.9 %copy-start.1 = (f32[8,2048]{1,0:T(8,128)S(1)}, f32[8,2048]{1,0:T(8,128)}, u32[]{:S(2)}) copy-start(f32[8,2048]{1,0:T(8,128)} %refs_5_.3) | copy-start | bytes 196612

commit v2 on v1

--- a/solution.py
+++ b/solution.py
@@ -14,7 +14,8 @@
 SUPPORT = 16
 LANES = 128
 ACROSS = GRID // FACET
-GROUPS = 5
+GROUPS = 6
+BACK = FROWS + 1
 GAIN_STEP = 0.5
 
 F32 = jnp.float32
@@ -69,7 +70,13 @@
 def layout_of(cap):
     lane_groups = LANES // cap
     row_blocks = -(-GROUPS // lane_groups)
-    return lane_groups, row_blocks, FROWS + 8 * row_blocks
+    rows = 8 * row_blocks - (6 if row_blocks == 3 else 0)
+    return lane_groups, row_blocks, FROWS + rows
+
+
+def read_block(ref, start, rows):
+    block = ref[start : start + rows, :]
+    return block if rows == 8 else jnp.concatenate([block, jnp.zeros((8 - rows, LANES), F32)], axis=0)
 
 
 def slot_parts(owner_row, count):
@@ -80,24 +87,34 @@
     return hits, jnp.sum(before * hits, axis=0, keepdims=True).astype(I32)
 
 
-def splat_rows(corner_ref, target_ref, start, count, step):
+def splat_rows(corner_ref, target_ref, start, count):
     for s in range(count):
-        target_ref[pl.ds(start + s, 1), :] = jnp.full((1, LANES), corner_ref[step * s], I32)
+        target_ref[start + s : start + s + 1, :] = jnp.full((1, LANES), corner_ref[0, s], I32)
 
 
 def send_kernel(
-    corner_ref, owner_ref, vis_ref, ku_ref, kv_ref, off_ref, image_ref,
-    send_ref, table_ref, freq_ref, mod_ref, *, count, cap,
+    corner_ref, owner_hbm, vis_hbm, ku_hbm, kv_hbm, off_hbm, image_hbm,
+    send_ref, table_ref, hits_ref, rank_ref,
+    owner_ref, vis_ref, ku_ref, kv_ref, off_ref, image_ref, freq_ref, mod_ref, sem_ref, *, count, cap,
 ):
     lane_groups, row_blocks, piece = layout_of(cap)
+    sources = [image_hbm, owner_hbm, vis_hbm, ku_hbm, kv_hbm, off_hbm]
+    targets = [image_ref, owner_ref, vis_ref, ku_ref, kv_ref, off_ref]
+    copies = [
+        pltpu.make_async_copy(src, dst, sem_ref.at[i]) for i, (src, dst) in enumerate(zip(sources, targets))
+    ]
+    for copy in copies:
+        copy.start()
     facet = lax.axis_index("facet")
     x_start = facet % ACROSS * FACET - GRID // 2
-    splat_rows(corner_ref, freq_ref, 0, count, 2)
+    splat_rows(corner_ref, freq_ref, 0, count)
     freq = freq_ref[...]
     cos_t, sin_t = phase_rows(iota((SUB, LANES), 0))
     table = jnp.concatenate([cos_t, sin_t], axis=0).astype(BF16)
     table_ref[...] = table
     cos_u, sin_u = phase_rows(freq)
+    for copy in copies:
+        copy.wait()
     image = image_ref[...]
     for s in range(count):
         both = jnp.concatenate([image * cos_u[s : s + 1], -image * sin_u[s : s + 1]], axis=0)
@@ -118,24 +135,23 @@
     owner_row = owner_ref[...]
     rows = owner_row.shape[1]
     hits, rank = slot_parts(owner_row, count)
-    blank = jnp.zeros((4, rows), F32)
-    misc = jnp.concatenate([vis_ref[...], off_ref[...].astype(F32), blank], axis=0)
-    parts = [ku_ref[0:8, :], ku_ref[8:16, :], kv_ref[0:8, :], kv_ref[8:16, :], misc]
-    total = jnp.zeros((count * row_blocks * 8, LANES), F32)
-    for group in range(lane_groups):
+    hits_ref[...] = hits
+    rank_ref[...] = rank
+    blank = jnp.zeros((6, rows), F32)
+    vis = jnp.concatenate([vis_ref[...], blank], axis=0)
+    offset = jnp.concatenate([off_ref[...].astype(F32), blank], axis=0)
+    parts = [ku_ref[0:8, :], ku_ref[8:16, :], vis, kv_ref[0:8, :], kv_ref[8:16, :], offset]
+    total = None
+    for group in range(-(-GROUPS // row_blocks)):
         mine = parts[group * row_blocks : (group + 1) * row_blocks]
-        if not mine:
-            continue
-        if len(mine) < row_blocks:
-            mine = mine + [jnp.zeros((8, rows), F32)] * (row_blocks - len(mine))
         stacked = jnp.concatenate(mine, axis=0)
         masked = jnp.concatenate([stacked * hits[s : s + 1] for s in range(count)], axis=0)
         place = (iota((LANES, rows), 0) == rank + group * cap).astype(F32)
-        total = total + dot_nt(masked, place, exact_products)
+        moved = dot_nt(masked, place, exact_products)
+        total = moved if total is None else total + moved
     for s in range(count):
-        send_ref[piece * s + FROWS : piece * (s + 1), :] = total[
-            8 * row_blocks * s : 8 * row_blocks * (s + 1)
-        ]
+        at = 8 * row_blocks * s
+        send_ref[piece * s + FROWS : piece * (s + 1), :] = total[at : at + piece - FROWS]
 
 
 def place_kernel(taps, offset):
@@ -177,7 +193,7 @@
 ):
     lane_groups, row_blocks, piece = layout_of(cap)
     height = count // ACROSS * FROWS
-    v_start = corner_ref[2 * lax.axis_index("facet") + 1]
+    v_start = corner_ref[1, lax.axis_index("facet")]
     sums = []
     for down in range(count // ACROSS):
         total = got_ref[piece * down * ACROSS : piece * down * ACROSS + FROWS, :]
@@ -195,17 +211,17 @@
             block, group = k % row_blocks, k // row_blocks
             value = None
             for j in range(lane_groups):
-                at = piece * (tile * lane_groups + j) + FROWS + 8 * block
-                moved = got_ref[at : at + 8, :]
+                at = FROWS + 8 * block
+                moved = read_block(got_ref, piece * (tile * lane_groups + j) + at, min(8, piece - at))
                 shift = (j - group) * cap % LANES
                 if shift:
                     moved = pltpu.roll(moved, shift, 1)
                 value = moved if value is None else jnp.where(lane_group == j, moved, value)
             found.append(value)
-        misc = found[4]
-        u_list.append(place_kernel(jnp.concatenate(found[0:2], axis=0), misc[2:3].astype(I32)))
-        v_list.append(place_kernel(jnp.concatenate(found[2:4], axis=0), misc[3:4].astype(I32)))
-        vis_list.append(misc)
+        offset = found[5].astype(I32)
+        u_list.append(place_kernel(jnp.concatenate(found[0:2], axis=0), offset[0:1]))
+        v_list.append(place_kernel(jnp.concatenate(found[3:5], axis=0), offset[1:2]))
+        vis_list.append(found[2])
     kern_u = jnp.concatenate(u_list, axis=1)
     kern_v = jnp.concatenate(v_list, axis=1)
     vis = jnp.concatenate(vis_list, axis=1)
@@ -226,10 +242,15 @@
 def group_corner(corner_ref, near_refs, group, groups, index):
     refs = [corner_ref] + list(near_refs)
     back = (lax.axis_index("freq") - group) % groups
-    value = refs[0][2 * index]
+    value = refs[0][0, index]
     for k in range(1, groups):
-        value = jnp.where(back == k, refs[k][2 * index], value)
+        value = jnp.where(back == k, refs[k][0, index], value)
     return value
+
+
+def turn(value, shift):
+    shift = shift % LANES
+    return pltpu.roll(value, shift, 1) if shift else value
 
 
 def second_kernel(*refs, count, cap, groups, scale):
@@ -237,7 +258,7 @@
     all_ref, own_ref, col_ref, ku_ref, kh_ref, vis_ref, back_ref, sum_ref = refs[groups:]
     lane_groups = LANES // cap
     height = col_ref.shape[0]
-    u_start = corner_ref[2 * lax.axis_index("facet")]
+    u_start = corner_ref[0, lax.axis_index("facet")]
     sum_ref[...] = jnp.zeros_like(sum_ref)
     row, col = iota((LANES, LANES), 0), iota((LANES, LANES), 1)
     same = (row < SUB) == (col < SUB)
@@ -264,60 +285,66 @@
     kern_u, kern_h = ku_ref[...], kh_ref[...]
     res_re, res_im = predict(columns, kern_u, kern_h, vis_ref[...], scale)
     rows = own_ref[...] + grid_rows(res_re, res_im, kern_u, kern_h)
-    res = jnp.concatenate([res_re, res_im, jnp.zeros((6, res_re.shape[1]), F32)], axis=0)
+    tiles = count // lane_groups
+    res_re = jnp.concatenate([res_re[:, LANES * t : LANES * (t + 1)] for t in range(tiles)], axis=0)
+    res_im = jnp.concatenate([res_im[:, LANES * t : LANES * (t + 1)] for t in range(tiles)], axis=0)
+    low = iota((tiles, LANES), 1) < cap
+    back = [
+        jnp.where(low, turn(res_re, -j * cap), turn(res_im, (1 - j) * cap)) for j in range(lane_groups)
+    ]
     for s in range(count):
-        tile, j = s // lane_groups, s % lane_groups
-        block = res[:, LANES * tile : LANES * (tile + 1)]
-        if j:
-            block = pltpu.roll(block, LANES - j * cap, 1)
-        down = s // ACROSS
+        tile, j, down = s // lane_groups, s % lane_groups, s // ACROSS
         for g in range(groups):
-            at = 16 * (g * count + s)
+            at = BACK * (g * count + s)
             back_ref[at : at + 8, :] = rows[8 * down : 8 * down + 8]
-            back_ref[at + 8 : at + 16, :] = block
-
-
-def image_kernel(*refs, count, groups, scale):
+            back_ref[at + 8 : at + 9, :] = back[j][tile : tile + 1]
+
+
+def phase_kernel(*refs, count, groups):
     corner_ref, near_refs = refs[0], refs[1:groups]
-    got_ref, table_ref, owner_ref, image_ref, out_ref, res_ref, freq_ref = refs[groups:]
-    total = groups * count
-    facet = lax.axis_index("facet")
-    x_start = facet % ACROSS * FACET - GRID // 2
+    cos_ref, sin_ref, cos_x_ref, sin_x_ref, freq_ref = refs[groups:]
+    x_start = lax.axis_index("facet") % ACROSS * FACET - GRID // 2
     for g in range(groups):
         for s in range(count):
-            d = g * count + s
             u_other = group_corner(corner_ref, near_refs, g, groups, s)
-            freq_ref[d : d + 1, :] = jnp.full((1, LANES), u_other, I32)
+            freq_ref[g * count + s : g * count + s + 1, :] = jnp.full((1, LANES), u_other, I32)
     freq = freq_ref[...]
+    cos_x, sin_x = phase_pair((freq + (iota(freq.shape, 1) & (SUB - 1))) * x_start)
+    cos_x_ref[...] = cos_x
+    sin_x_ref[...] = jnp.where(iota(freq.shape, 1) < SUB, -sin_x, sin_x)
+    cos_ref[...], sin_ref[...] = phase_rows(freq)
+
+
+def image_kernel(
+    got_ref, table_ref, cos_ref, sin_ref, cos_x_ref, sin_x_ref, hits_ref, rank_ref, image_ref,
+    out_ref, res_ref, *, count, groups, cap, scale,
+):
+    total = groups * count
     low = iota((FROWS, LANES), 1) < SUB
-    cos_x, sin_x = phase_pair((freq + (iota(freq.shape, 1) & (SUB - 1))) * x_start)
-    sin_x = jnp.where(iota(freq.shape, 1) < SUB, -sin_x, sin_x)
+    cos_x, sin_x = cos_x_ref[...], sin_x_ref[...]
     left = []
     for d in range(total):
-        block = got_ref[16 * d : 16 * d + 8, :]
+        block = got_ref[BACK * d : BACK * d + 8, :]
         moved = block * cos_x[d : d + 1] + pltpu.roll(block, SUB, 1) * sin_x[d : d + 1]
         left.append(jnp.where(low, moved, -moved))
         left.append(pltpu.roll(moved, SUB, 1))
     left = jnp.concatenate(left, axis=0).astype(BF16)
-    cos_u, sin_u = phase_rows(freq)
     both = dot_nn(left, table_ref[...])
     dirty = jnp.zeros((FROWS, FACET), F32)
     for d in range(total):
-        dirty = dirty + both[16 * d : 16 * d + 8] * cos_u[d : d + 1]
-        dirty = dirty - both[16 * d + 8 : 16 * d + 16] * sin_u[d : d + 1]
+        dirty = dirty + both[16 * d : 16 * d + 8] * cos_ref[d : d + 1, :]
+        dirty = dirty - both[16 * d + 8 : 16 * d + 16] * sin_ref[d : d + 1, :]
     out_ref[...] = image_ref[...] + (GAIN_STEP * scale) * dirty
 
-    owner_row = owner_ref[...]
-    rows = owner_row.shape[1]
-    hits, rank = slot_parts(owner_row, count)
-    first = lax.axis_index("freq") * (count * 16)
-    back = [got_ref[pl.ds(pl.multiple_of(first + 16 * s + 8, 8), 8), :] for s in range(count)]
-    place = (iota((LANES, rows), 0) == rank).astype(F32)
-    found = dot_nn(jnp.concatenate(back, axis=0), place, exact_products)
-    picked = jnp.zeros((8, rows), F32)
-    for s in range(count):
-        picked = picked + found[8 * s : 8 * s + 8] * hits[s : s + 1]
-    res_ref[...] = picked[0:2]
+    rows = rank_ref.shape[1]
+    first = lax.axis_index("freq") * (count * BACK) + 8
+    back = jnp.concatenate([got_ref[pl.ds(first + BACK * s, 1), :] for s in range(count)], axis=0)
+    picked = []
+    for part in range(2):
+        place = (iota((LANES, rows), 0) == rank_ref[...] + part * cap).astype(F32)
+        found = dot_nn(back, place, exact_products)
+        picked.append(jnp.sum(found * hits_ref[...], axis=0, keepdims=True))
+    res_ref[...] = jnp.concatenate(picked, axis=0)
 
 
 def on_device(model_image, visibilities, kernel_u, kernel_v, owners, offsets, corners):
@@ -325,13 +352,13 @@
     groups = lax.axis_size("freq")
     rows = owners.shape[0]
     cap = 4 * rows // count
-    assert count % ACROSS == 0 and LANES % cap == 0
+    assert count % ACROSS == 0 and 2 * cap <= LANES and LANES % cap == 0
     scale = 1.0 / math.sqrt(count * FROWS * FACET)
     lane_groups, row_blocks, piece = layout_of(cap)
     height = count // ACROSS * FROWS
     slots = count * cap
     total = groups * count
-    corner = corners.reshape(2 * count)
+    corner = corners[0].T
     near = [
         lax.ppermute(corner, "freq", [(g, (g + k) % groups) for g in range(groups)])
         for k in range(1, groups)
@@ -339,33 +366,50 @@
     owner_row = owners.reshape(1, rows)
     smem = pl.BlockSpec(memory_space=pltpu.SMEM)
     vmem = pl.BlockSpec(memory_space=pltpu.VMEM)
+    far = pl.BlockSpec(memory_space=pltpu.HBM)
     params = pltpu.CompilerParams(vmem_limit_bytes=48 * 1024 * 1024)
 
     def shape(*dims, dtype=F32):
         return jax.ShapeDtypeStruct(dims, dtype)
 
-    def call(body, out_shape, scalars, arrays, name, scratch=(), **sizes):
+    def call(body, out_shape, scalars, arrays, name, scratch=(), space=vmem, **sizes):
         return pl.pallas_call(
             lambda *refs: body(*refs, **sizes),
             out_shape=out_shape,
-            in_specs=[smem] * len(scalars) + [vmem] * len(arrays),
+            in_specs=[smem] * len(scalars) + [space] * len(arrays),
             out_specs=jax.tree.map(lambda _: vmem, out_shape),
             scratch_shapes=scratch,
             compiler_params=params,
             name=name,
         )(*scalars, *arrays)
 
-    send, table = call(
+    def exchange(block, axes, parts):
+        view = block.reshape(parts, 1, block.size // parts)
+        return lax.all_to_all(view, axes, split_axis=0, concat_axis=0, tiled=True).reshape(block.shape)
+
+    inputs = [owner_row, visibilities, kernel_u, kernel_v, offsets]
+    send, table, hits, rank = call(
         send_kernel,
-        (shape(count * piece, LANES), shape(2 * SUB, FACET, dtype=BF16)),
+        (
+            shape(count * piece, LANES),
+            shape(2 * SUB, FACET, dtype=BF16),
+            shape(count, rows),
+            shape(1, rows, dtype=I32),
+        ),
         [corner],
-        [owner_row, visibilities, kernel_u, kernel_v, offsets, model_image],
+        [pltpu.with_memory_space_constraint(x, pltpu.HBM) for x in [*inputs, model_image]],
         "send_rows",
-        [pltpu.VMEM((count, LANES), I32), pltpu.VMEM((16 * count, FACET), BF16)],
+        [pltpu.VMEM(x.shape, x.dtype) for x in [*inputs, model_image]]
+        + [
+            pltpu.VMEM((count, LANES), I32),
+            pltpu.VMEM((16 * count, FACET), BF16),
+            pltpu.SemaphoreType.DMA((6,)),
+        ],
+        far,
         count=count,
         cap=cap,
     )
-    got = lax.all_to_all(send, "facet", split_axis=0, concat_axis=0, tiled=True)
+    got = exchange(send, "facet", count)
     columns, kern_u, kern_h, vis, spread, own = call(
         first_kernel,
         (
@@ -384,10 +428,20 @@
         groups=groups,
         scale=scale,
     )
-    everyone = lax.all_to_all(spread, ("freq", "facet"), split_axis=0, concat_axis=0, tiled=True)
+    everyone = exchange(spread, ("freq", "facet"), total)
+    phases = call(
+        phase_kernel,
+        (shape(total, FACET), shape(total, FACET), shape(total, LANES), shape(total, LANES)),
+        [corner, *near],
+        [],
+        "phases",
+        [pltpu.VMEM((total, LANES), I32)],
+        count=count,
+        groups=groups,
+    )
     back = call(
         second_kernel,
-        shape(total * 16, LANES),
+        shape(total * BACK, LANES),
         [corner, *near],
         [everyone, own, columns, kern_u, kern_h, vis],
         "second_cycle",
@@ -397,16 +451,16 @@
         groups=groups,
         scale=scale,
     )
-    returned = lax.all_to_all(back, ("freq", "facet"), split_axis=0, concat_axis=0, tiled=True)
+    returned = exchange(back, ("freq", "facet"), total)
     return call(
         image_kernel,
         (shape(FROWS, FACET), shape(2, rows)),
-        [corner, *near],
-        [returned, table, owner_row, model_image],
+        [],
+        [returned, table, *phases, hits, rank, model_image],
         "form_image",
-        [pltpu.VMEM((total, LANES), I32)],
         count=count,
         groups=groups,
+        cap=cap,
         scale=scale,
     )
 

time: 56.7 us -> 51.7 us (0.912)
  blocking collectives: 30.1 us -> 16.4 us
  waiting for transfers between devices: 8.42 us -> 16.1 us
  local copies, waits for them, and re-layouts: 3.76 us -> 0.68 us
  starting transfers between devices: 4.62 us -> 7.35 us
  Pallas kernels: 8.77 us -> 10.2 us
    all_to_all x2 -> x1, blocking collectives: 30.1 us -> 16.4 us  [exchange(): lax.all_to_all(view, axes, split_axis=0, concat_axis=0, tiled=True)]
    all_to_all x1 -> x2, waiting for transfers between devices: 6.41 us -> 14.1 us  [exchange(): lax.all_to_all(view, axes, split_axis=0, concat_axis=0, tiled=True)]
    unnamed x15 -> x4, local copies, waits for them, and re-layouts: 3.68 us -> 0.68 us
    all_to_all x1 -> x2, starting transfers between devices: 2.79 us -> 5.53 us  [exchange(): lax.all_to_all(view, axes, split_axis=0, concat_axis=0, tiled=True)]
    pallas_call x4 -> x5, Pallas kernels: 8.77 us -> 10.2 us  [call(): pl.pallas_call(lambda *refs: body(*refs, **sizes), out_shape=out_shape, i...]
  transfers between devices with their start and end apart: 2 -> 3, of which waited for: 2 -> 3; matrix products, arithmetic and copies ran while one was open for 0% -> 0% of each run, Pallas kernels for 0% -> 1%
where the time goes in v2:
time: 51.7 us; the launch traced here: 51.4 us
  blocking collectives  16.4 us (32%)
  waiting for transfers between devices  16.1 us (31%)
  Pallas kernels  10.2 us (20%)
  starting transfers between devices  7.35 us (14%)
  local copies, waits for them, and re-layouts  0.68 us (1%)
  between operations  0.67 us (1%)
    all_to_all x1, blocking collectives, exchange(): lax.all_to_all(view, axes, split_axis=0, concat_axis=0, tiled=True)  16.4 us
    all_to_all x2, waiting for transfers between devices, exchange(): lax.all_to_all(view, axes, split_axis=0, concat_axis=0, tiled=True)  14.1 us
    pallas_call x5, Pallas kernels, call(): pl.pallas_call(lambda *refs: body(*refs, **sizes), out_shape=out_shape, i...  10.2 us
    all_to_all x2, starting transfers between devices, exchange(): lax.all_to_all(view, axes, split_axis=0, concat_axis=0, tiled=True)  5.53 us
    ppermute x1, waiting for transfers between devices, on_device(): lax.ppermute(corner, 'freq', [(g, (g + k) % groups) for g in range(groups)])  1.97 us
    ppermute x1, starting transfers between devices, on_device(): lax.ppermute(corner, 'freq', [(g, (g + k) % groups) for g in range(groups)])  1.83 us
  transfers between devices with their start and end apart: 3, of which 3 were waited for; matrix products, arithmetic and copies ran while one was open for 0% of the time, Pallas kernels for 1%

profile of v2, /device:TPU:0, one launch (start us, length us, event | category | flops | bytes accessed | tf_op | source)
XLA Modules:
  0.0 51.4 jit_solution(3505849742756739485)
XLA Ops:
  0.6 0.0 copy-start.1
  0.6 0.7 %copy-done.1 = s32[1,16,2]{1,2,0:T(2,128)S(1)} copy-done((s32[1,16,2]{1,2,0:T(2,128)S(1)}, s32[1,16,2]{1,2,0:T(2,128)}, u32[]{:S(2)}) %copy-start.1) | copy-done | bytes 152
  1.3 2.7 %send_rows.1 = (f32[416,128]{1,0:T(8,128)S(1)}, bf16[128,2048]{1,0:T(8,128)(2,1)S(1)}, f32[16,256]{1,0:T(8,128)S(1)}, s32[1,256]{1,0:T(1,128)S(1)}) custom-call(s32[2,16]{1,0:T(2,128)S(1)} %bitcast.14, s32[1,256]{1,0:T(1,128)} %bitcast.19, f32[2,256]{1,0:T(2,128)} %refs_2_.1, f32[16,256]{1,0:T(8,128)} %refs_3_.1, f32[16,256]{1,0:T(8,128)} %refs_4_.1, ...), custom_call_target="tpu_custom_call" | custom-call | tf_op jit(solution)/shard_map/send_rows/pallas_call | solution.py:376
  4.0 16.4 %all_to_all.15 = f32[16,1,3328]{2,1,0:T(1,128)S(1)} all-to-all(f32[16,1,3328]{2,1,0:T(1,128)S(1)} %bitcast.13), channel_id=1, replica_groups=mesh['freq'=2,'facet'=16] {'facet'}, dimensions={0} | all-to-all | bytes 425984 | tf_op jit(solution)/shard_map/all_to_all | solution.py:388
  20.4 2.2 %first_cycle.1 = (f32[16,128]{1,0:T(8,128)S(1)}, f32[64,1024]{1,0:T(8,128)S(1)}, f32[32,1024]{1,0:T(8,128)S(1)}, f32[8,1024]{1,0:T(8,128)S(1)}, f32[512,128]{1,0:T(8,128)}, /*index=5*/f32[16,128]{1,0:T(8,128)S(1)}) custom-call(s32[2,16]{1,0:T(2,128)S(1)} %bitcast.15, f32[416,128]{1,0:T(8,128)S(1)} %bitcast.11), custom_call_target="tpu_custom_call" | custom-call | tf_op jit(solution)/shard_map/first_cycle/pallas_call | solution.py:376
  22.7 2.6 %all-to-all-start.1 = ((f32[32,1,2048]{2,1,0:T(1,128)}), f32[32,1,2048]{2,1,0:T(1,128)S(1)}, u32[]{:S(2)}, u32[]{:S(2)}) async-start(f32[32,1,2048]{2,1,0:T(1,128)} %bitcast.6), calls=%async_computation.1 | async-start | bytes 524288 | tf_op jit(solution)/shard_map/all_to_all | solution.py:388
  25.3 1.8 %collective-permute-start = (s32[2,16]{1,0:T(2,128)S(1)}, s32[2,16]{1,0:T(2,128)S(1)}, u32[]{:S(2)}, u32[]{:S(2)}) collective-permute-start(s32[2,16]{1,0:T(2,128)S(1)} %bitcast.16), channel_id=1, source_target_pairs={{0,16},{16,0},{1,17},{17,1},{2,18},{18,2},{3,19},{19,3},{4,20},{20... | collective-permute-start | bytes 392 | tf_op jit(solution)/shard_map/ppermute | solution.py:363
  27.1 2.0 %collective-permute-done.refs_1_ = s32[2,16]{1,0:T(2,128)S(1)} collective-permute-done((s32[2,16]{1,0:T(2,128)S(1)}, s32[2,16]{1,0:T(2,128)S(1)}, u32[]{:S(2)}, u32[]{:S(2)}) %collective-permute-start) | collective-permute-done | bytes 160 | tf_op jit(solution)/shard_map/ppermute | solution.py:363
  29.1 6.5 %all-to-all-done.1 = f32[32,1,2048]{2,1,0:T(1,128)S(1)} async-done(((f32[32,1,2048]{2,1,0:T(1,128)}), f32[32,1,2048]{2,1,0:T(1,128)S(1)}, u32[]{:S(2)}, u32[]{:S(2)}) %all-to-all-start.1) | async-done | bytes 262176 | tf_op jit(solution)/shard_map/all_to_all | solution.py:388
  35.5 3.0 %second_cycle.1 = f32[288,128]{1,0:T(8,128)} custom-call(s32[2,16]{1,0:T(2,128)S(1)} %bitcast.17, s32[2,16]{1,0:T(2,128)S(1)} %collective-permute-done.refs_1_, f32[512,128]{1,0:T(8,128)S(1)} %bitcast.10, f32[16,128]{1,0:T(8,128)S(1)} %get-tuple-element.18.refs_3_, f32[16,128]{1,0:T(8,128)S(1)} %get-tuple-element.19.refs_4_, ...), custom_call_target="tpu_custom_call" | custom-call | tf_op jit(solution)/shard_map/second_cycle/pallas_call | solution.py:376
  38.5 0.0 copy-start
  38.5 2.9 %all-to-all-start.2 = ((f32[32,1,1152]{2,1,0:T(1,128)}), f32[32,1,1152]{2,1,0:T(1,128)S(1)}, u32[]{:S(2)}, u32[]{:S(2)}) async-start(f32[32,1,1152]{2,1,0:T(1,128)} %bitcast.8), calls=%async_computation.2 | async-start | bytes 294912 | tf_op jit(solution)/shard_map/all_to_all | solution.py:388
  41.4 0.7 %phases.1 = (f32[32,2048]{1,0:T(8,128)S(1)}, f32[32,2048]{1,0:T(8,128)S(1)}, f32[32,128]{1,0:T(8,128)S(1)}, f32[32,128]{1,0:T(8,128)S(1)}) custom-call(s32[2,16]{1,0:T(2,128)S(1)} %bitcast.18, s32[2,16]{1,0:T(2,128)S(1)} %collective-permute-done.refs_1_), custom_call_target="tpu_custom_call" | custom-call | tf_op jit(solution)/shard_map/phases/pallas_call | solution.py:376
  42.1 7.7 %all-to-all-done.2 = f32[32,1,1152]{2,1,0:T(1,128)S(1)} async-done(((f32[32,1,1152]{2,1,0:T(1,128)}), f32[32,1,1152]{2,1,0:T(1,128)S(1)}, u32[]{:S(2)}, u32[]{:S(2)}) %all-to-all-start.2) | async-done | bytes 147488 | tf_op jit(solution)/shard_map/all_to_all | solution.py:388
  49.8 0.0 copy-done
  49.8 1.6 %form_image.1 = (f32[8,2048]{1,0:T(8,128)}, f32[2,256]{1,0:T(2,128)}) custom-call(f32[288,128]{1,0:T(8,128)S(1)} %bitcast.12, bf16[128,2048]{1,0:T(8,128)(2,1)S(1)} %get-tuple-element.23.refs_1_, f32[32,2048]{1,0:T(8,128)S(1)} %get-tuple-element.24.refs_2_, f32[32,2048]{1,0:T(8,128)S(1)} %get-tuple-element.25.refs_3_, ...), custom_call_target="tpu_custom_call" | custom-call | tf_op jit(solution)/shard_map/form_image/pallas_call | solution.py:376
Async XLA Ops:
  0.6 0.7 %copy-start.1 = (s32[1,16,2]{1,2,0:T(2,128)S(1)}, s32[1,16,2]{1,2,0:T(2,128)}, u32[]{:S(2)}) copy-start(s32[1,16,2]{1,2,0:T(2,128)} %param.13) | copy-start | bytes 388
  22.7 12.9 %all-to-all-start.1 = ((f32[32,1,2048]{2,1,0:T(1,128)}), f32[32,1,2048]{2,1,0:T(1,128)S(1)}, u32[]{:S(2)}, u32[]{:S(2)}) async-start(f32[32,1,2048]{2,1,0:T(1,128)} %bitcast.6), calls=%async_computation.1 | async-start | bytes 524288 | tf_op jit(solution)/shard_map/all_to_all | solution.py:388
  25.3 3.8 %collective-permute-start = (s32[2,16]{1,0:T(2,128)S(1)}, s32[2,16]{1,0:T(2,128)S(1)}, u32[]{:S(2)}, u32[]{:S(2)}) collective-permute-start(s32[2,16]{1,0:T(2,128)S(1)} %bitcast.16), channel_id=1, source_target_pairs={{0,16},{16,0},{1,17},{17,1},{2,18},{18,2},{3,19},{19,3},{4,20},{20... | collective-permute-start | bytes 392 | tf_op jit(solution)/shard_map/ppermute | solution.py:363
  38.5 11.4 %copy-start = (f32[8,2048]{1,0:T(8,128)S(1)}, f32[8,2048]{1,0:T(8,128)}, u32[]{:S(2)}) copy-start(f32[8,2048]{1,0:T(8,128)} %refs_8_.1) | copy-start | bytes 196612
  38.5 11.4 %all-to-all-start.2 = ((f32[32,1,1152]{2,1,0:T(1,128)}), f32[32,1,1152]{2,1,0:T(1,128)S(1)}, u32[]{:S(2)}, u32[]{:S(2)}) async-start(f32[32,1,1152]{2,1,0:T(1,128)} %bitcast.8), calls=%async_computation.2 | async-start | bytes 294912 | tf_op jit(solution)/shard_map/all_to_all | solution.py:388

commit v3 on v2

--- a/solution.py
+++ b/solution.py
@@ -67,6 +67,20 @@
     )
 
 
+def split(value):
+    high = value.astype(BF16)
+    return jnp.concatenate([high, (value - high.astype(F32)).astype(BF16)], axis=0)
+
+
+def fold(value):
+    half = value.shape[0] // 2
+    return value[:half] + value[half:]
+
+
+def spread_row(ref, row):
+    return ref[pl.ds(row, FROWS, stride=0), :]
+
+
 def layout_of(cap):
     lane_groups = LANES // cap
     row_blocks = -(-GROUPS // lane_groups)
@@ -87,19 +101,15 @@
     return hits, jnp.sum(before * hits, axis=0, keepdims=True).astype(I32)
 
 
-def splat_rows(corner_ref, target_ref, start, count):
-    for s in range(count):
-        target_ref[start + s : start + s + 1, :] = jnp.full((1, LANES), corner_ref[0, s], I32)
-
-
 def send_kernel(
-    corner_ref, owner_hbm, vis_hbm, ku_hbm, kv_hbm, off_hbm, image_hbm,
-    send_ref, table_ref, hits_ref, rank_ref,
-    owner_ref, vis_ref, ku_ref, kv_ref, off_ref, image_ref, freq_ref, mod_ref, sem_ref, *, count, cap,
+    corner_hbm, owner_hbm, vis_hbm, ku_hbm, kv_hbm, off_hbm, image_hbm,
+    send_ref, table_ref, hits_ref, rank_ref, corner_out,
+    corner_ref, owner_ref, vis_ref, ku_ref, kv_ref, off_ref, image_ref,
+    freq_ref, cos_ref, sin_ref, mod_ref, sem_ref, *, count, cap,
 ):
     lane_groups, row_blocks, piece = layout_of(cap)
-    sources = [image_hbm, owner_hbm, vis_hbm, ku_hbm, kv_hbm, off_hbm]
-    targets = [image_ref, owner_ref, vis_ref, ku_ref, kv_ref, off_ref]
+    sources = [corner_hbm, image_hbm, owner_hbm, vis_hbm, ku_hbm, kv_hbm, off_hbm, corner_hbm]
+    targets = [corner_ref, image_ref, owner_ref, vis_ref, ku_ref, kv_ref, off_ref, corner_out]
     copies = [
         pltpu.make_async_copy(src, dst, sem_ref.at[i]) for i, (src, dst) in enumerate(zip(sources, targets))
     ]
@@ -107,17 +117,19 @@
         copy.start()
     facet = lax.axis_index("facet")
     x_start = facet % ACROSS * FACET - GRID // 2
-    splat_rows(corner_ref, freq_ref, 0, count)
-    freq = freq_ref[...]
     cos_t, sin_t = phase_rows(iota((SUB, LANES), 0))
     table = jnp.concatenate([cos_t, sin_t], axis=0).astype(BF16)
     table_ref[...] = table
-    cos_u, sin_u = phase_rows(freq)
-    for copy in copies:
+    copies[0].wait()
+    for s in range(count):
+        freq_ref[s : s + 1, :] = jnp.full((1, LANES), corner_ref[0, s], I32)
+    freq = freq_ref[...]
+    cos_ref[...], sin_ref[...] = phase_rows(freq)
+    for copy in copies[1:]:
         copy.wait()
     image = image_ref[...]
     for s in range(count):
-        both = jnp.concatenate([image * cos_u[s : s + 1], -image * sin_u[s : s + 1]], axis=0)
+        both = jnp.concatenate([image * spread_row(cos_ref, s), -image * spread_row(sin_ref, s)], axis=0)
         mod_ref[16 * s : 16 * s + 16, :] = both.astype(BF16)
     prod = dot_nt(mod_ref[...], table)
     lane = iota((FROWS, LANES), 1)
@@ -141,17 +153,25 @@
     vis = jnp.concatenate([vis_ref[...], blank], axis=0)
     offset = jnp.concatenate([off_ref[...].astype(F32), blank], axis=0)
     parts = [ku_ref[0:8, :], ku_ref[8:16, :], vis, kv_ref[0:8, :], kv_ref[8:16, :], offset]
-    total = None
-    for group in range(-(-GROUPS // row_blocks)):
+    parts = parts + [jnp.zeros((8, rows), F32)] * (-len(parts) % row_blocks)
+    groups = len(parts) // row_blocks
+    high = 16 * -(-row_blocks // 2)
+    left, places = [], []
+    for group in range(groups):
         mine = parts[group * row_blocks : (group + 1) * row_blocks]
-        stacked = jnp.concatenate(mine, axis=0)
-        masked = jnp.concatenate([stacked * hits[s : s + 1] for s in range(count)], axis=0)
-        place = (iota((LANES, rows), 0) == rank + group * cap).astype(F32)
-        moved = dot_nt(masked, place, exact_products)
-        total = moved if total is None else total + moved
+        mine = mine + [jnp.zeros((8, rows), F32)] * (high // 8 - row_blocks)
+        both = split(jnp.concatenate(mine, axis=0))
+        place = (iota((LANES, rows), 0) == rank + group * cap).astype(F32).astype(BF16)
+        left += [both[:high], both[high:]]
+        places += [place, place]
+    stacked = jnp.concatenate(left, axis=1)
+    wide = jnp.concatenate([hits] * (2 * groups), axis=1)
+    masked = [
+        stacked * jnp.broadcast_to(wide[s : s + 1], stacked.shape).astype(BF16) for s in range(count)
+    ]
+    total = dot_nt(jnp.concatenate(masked, axis=0), jnp.concatenate(places, axis=1))
     for s in range(count):
-        at = 8 * row_blocks * s
-        send_ref[piece * s + FROWS : piece * (s + 1), :] = total[at : at + piece - FROWS]
+        send_ref[piece * s + FROWS : piece * (s + 1), :] = total[high * s : high * s + piece - FROWS]
 
 
 def place_kernel(taps, offset):
@@ -169,10 +189,12 @@
     return jnp.concatenate(blocks, axis=0)
 
 
-def predict(column_rows, kern_u, kern_h, vis, scale):
-    height = column_rows.shape[0]
-    stacked = jnp.concatenate([column_rows[:, :SUB], column_rows[:, SUB:]], axis=0)
-    partial = dot_nn(stacked, kern_u, exact_products)
+def predict(columns, kern_u, kern_h, vis, scale):
+    height = columns.shape[0]
+    low = iota(columns.shape, 1) < SUB
+    turned = pltpu.roll(columns, SUB, 1)
+    twice = jnp.concatenate([jnp.where(low, columns, turned), jnp.where(low, turned, columns)], axis=0)
+    partial = fold(dot_nn(split(twice), kern_u))
     part_re, part_im = partial[:height], partial[height:]
     h_re, h_im = kern_h[:height], kern_h[height:]
     pred_re = jnp.sum(h_re * part_re - h_im * part_im, axis=0, keepdims=True)
@@ -183,9 +205,10 @@
 def grid_rows(res_re, res_im, kern_u, kern_h):
     height = kern_h.shape[0] // 2
     h_re, h_im = kern_h[:height], kern_h[height:]
-    spread = jnp.concatenate([h_re * res_re + h_im * res_im, h_re * res_im - h_im * res_re], axis=0)
-    rows = dot_nt(spread, kern_u, exact_products)
-    return jnp.concatenate([rows[:height], rows[height:]], axis=1)
+    weighted = jnp.concatenate([h_re * res_re + h_im * res_im, h_re * res_im - h_im * res_re], axis=0)
+    rows = fold(dot_nt(split(weighted), kern_u))
+    rows = rows + pltpu.roll(rows, SUB, 1)
+    return jnp.where(iota((height, LANES), 1) < SUB, rows[:height], rows[height:])
 
 
 def first_kernel(
@@ -225,10 +248,11 @@
     kern_u = jnp.concatenate(u_list, axis=1)
     kern_v = jnp.concatenate(v_list, axis=1)
     vis = jnp.concatenate(vis_list, axis=1)
-    row = iota((height, SUB), 0)
+    row = iota((height, LANES), 0)
     y_pos = row // FROWS * FACET - GRID // 2 + row % FROWS
-    cos_y, sin_y = phase_pair((v_start + iota((height, SUB), 1)) * y_pos)
-    kern_h = dot_nn(jnp.concatenate([cos_y, -sin_y], axis=0), kern_v, exact_products)
+    cos_y, sin_y = phase_pair((v_start + (iota((height, LANES), 1) & (SUB - 1))) * y_pos)
+    kern_h = fold(dot_nn(split(jnp.concatenate([cos_y, -sin_y], axis=0)), split(kern_v)))
+    kern_u = split(kern_u)
     ku_ref[...] = kern_u
     kh_ref[...] = kern_h
     vis_ref[...] = vis
@@ -253,35 +277,28 @@
     return pltpu.roll(value, shift, 1) if shift else value
 
 
-def second_kernel(*refs, count, cap, groups, scale):
-    corner_ref, near_refs = refs[0], refs[1:groups]
-    all_ref, own_ref, col_ref, ku_ref, kh_ref, vis_ref, back_ref, sum_ref = refs[groups:]
+def second_kernel(
+    all_ref, select_ref, own_ref, col_ref, ku_ref, kh_ref, vis_ref, back_ref, *, count, cap, groups, scale,
+):
     lane_groups = LANES // cap
     height = col_ref.shape[0]
-    u_start = corner_ref[0, lax.axis_index("facet")]
-    sum_ref[...] = jnp.zeros_like(sum_ref)
-    row, col = iota((LANES, LANES), 0), iota((LANES, LANES), 1)
-    same = (row < SUB) == (col < SUB)
-    row_a, col_a = row & (SUB - 1), col & (SUB - 1)
-    sign = jnp.where(col < SUB, 1.0, -1.0)
-    half = GRID // 2
-
-    def overlap(d, carry):
-        u_other = group_corner(corner_ref, near_refs, d // count, groups, d % count)
-        ahead = ((u_start - u_other + half) & (GRID - 1)) - half
-        mirror = (-u_start - u_other) & (GRID - 1)
-
-        @pl.when(((ahead > -SUB) & (ahead < SUB)) | (mirror < 2 * SUB - 1))
-        def _():
-            select = jnp.where(same & (row_a == col_a + ahead), 1.0, 0.0)
-            select = select + jnp.where(same & (row_a + col_a == mirror), sign, 0.0)
-            block = all_ref[pl.ds(pl.multiple_of(d * height, 8), height), :]
-            sum_ref[...] += dot_nn(block, select, exact_products)
-
-        return carry
-
-    lax.fori_loop(0, groups * count, overlap, 0)
-    columns = col_ref[...] + (GAIN_STEP * scale * (GRID / 2)) * sum_ref[...]
+    total = groups * count
+    chunk = math.gcd(total, 32)
+
+    def overlap(part, carry):
+        blocks = []
+        for d in range(chunk):
+            at = pl.multiple_of((part * chunk + d) * height, 8)
+            blocks.append(split(all_ref[pl.ds(at, height), :]))
+        at = pl.multiple_of(part * chunk * LANES, LANES)
+        return carry + dot_nn(jnp.concatenate(blocks, axis=1), select_ref[pl.ds(at, chunk * LANES), :])
+
+    extra = jnp.zeros((2 * height, LANES), F32)
+    if total == chunk:
+        extra = overlap(0, extra)
+    else:
+        extra = lax.fori_loop(0, total // chunk, overlap, extra)
+    columns = col_ref[...] + (GAIN_STEP * scale * (GRID / 2)) * fold(extra)
     kern_u, kern_h = ku_ref[...], kh_ref[...]
     res_re, res_im = predict(columns, kern_u, kern_h, vis_ref[...], scale)
     rows = own_ref[...] + grid_rows(res_re, res_im, kern_u, kern_h)
@@ -300,14 +317,30 @@
             back_ref[at + 8 : at + 9, :] = back[j][tile : tile + 1]
 
 
-def phase_kernel(*refs, count, groups):
+def prepare_kernel(*refs, count, groups):
     corner_ref, near_refs = refs[0], refs[1:groups]
-    cos_ref, sin_ref, cos_x_ref, sin_x_ref, freq_ref = refs[groups:]
-    x_start = lax.axis_index("facet") % ACROSS * FACET - GRID // 2
-    for g in range(groups):
-        for s in range(count):
-            u_other = group_corner(corner_ref, near_refs, g, groups, s)
-            freq_ref[g * count + s : g * count + s + 1, :] = jnp.full((1, LANES), u_other, I32)
+    cos_ref, sin_ref, cos_x_ref, sin_x_ref, select_ref, freq_ref = refs[groups:]
+    facet = lax.axis_index("facet")
+    x_start = facet % ACROSS * FACET - GRID // 2
+    u_start = corner_ref[0, facet]
+    row, col = iota((LANES, LANES), 0), iota((LANES, LANES), 1)
+    same = (row < SUB) == (col < SUB)
+    row_a, col_a = row & (SUB - 1), col & (SUB - 1)
+    behind = jnp.where(same, row_a - col_a, GRID)
+    across = jnp.where(same, row_a + col_a, GRID)
+    sign = jnp.where(col < SUB, 1.0, -1.0)
+    half = GRID // 2
+
+    def fill(d, carry):
+        u_other = group_corner(corner_ref, near_refs, d // count, groups, d % count)
+        freq_ref[pl.ds(d, 1), :] = jnp.full((1, LANES), u_other, I32)
+        ahead = ((u_start - u_other + half) & (GRID - 1)) - half
+        mirror = (-u_start - u_other) & (GRID - 1)
+        select = jnp.where(behind == ahead, 1.0, 0.0) + jnp.where(across == mirror, sign, 0.0)
+        select_ref[pl.ds(pl.multiple_of(d * LANES, LANES), LANES), :] = select.astype(BF16)
+        return carry
+
+    lax.fori_loop(0, groups * count, fill, 0)
     freq = freq_ref[...]
     cos_x, sin_x = phase_pair((freq + (iota(freq.shape, 1) & (SUB - 1))) * x_start)
     cos_x_ref[...] = cos_x
@@ -332,8 +365,8 @@
     both = dot_nn(left, table_ref[...])
     dirty = jnp.zeros((FROWS, FACET), F32)
     for d in range(total):
-        dirty = dirty + both[16 * d : 16 * d + 8] * cos_ref[d : d + 1, :]
-        dirty = dirty - both[16 * d + 8 : 16 * d + 16] * sin_ref[d : d + 1, :]
+        dirty = dirty + both[16 * d : 16 * d + 8] * spread_row(cos_ref, d)
+        dirty = dirty - both[16 * d + 8 : 16 * d + 16] * spread_row(sin_ref, d)
     out_ref[...] = image_ref[...] + (GAIN_STEP * scale) * dirty
 
     rows = rank_ref.shape[1]
@@ -359,10 +392,6 @@
     slots = count * cap
     total = groups * count
     corner = corners[0].T
-    near = [
-        lax.ppermute(corner, "freq", [(g, (g + k) % groups) for g in range(groups)])
-        for k in range(1, groups)
-    ]
     owner_row = owners.reshape(1, rows)
     smem = pl.BlockSpec(memory_space=pltpu.SMEM)
     vmem = pl.BlockSpec(memory_space=pltpu.VMEM)
@@ -387,34 +416,42 @@
         view = block.reshape(parts, 1, block.size // parts)
         return lax.all_to_all(view, axes, split_axis=0, concat_axis=0, tiled=True).reshape(block.shape)
 
-    inputs = [owner_row, visibilities, kernel_u, kernel_v, offsets]
-    send, table, hits, rank = call(
+    inputs = [corner, owner_row, visibilities, kernel_u, kernel_v, offsets, model_image]
+    send, table, hits, rank, corner = call(
         send_kernel,
         (
             shape(count * piece, LANES),
             shape(2 * SUB, FACET, dtype=BF16),
             shape(count, rows),
             shape(1, rows, dtype=I32),
+            shape(*corner.shape, dtype=I32),
         ),
-        [corner],
-        [pltpu.with_memory_space_constraint(x, pltpu.HBM) for x in [*inputs, model_image]],
+        [],
+        [pltpu.with_memory_space_constraint(x, pltpu.HBM) for x in inputs],
         "send_rows",
-        [pltpu.VMEM(x.shape, x.dtype) for x in [*inputs, model_image]]
+        [pltpu.SMEM(corner.shape, I32)]
+        + [pltpu.VMEM(x.shape, x.dtype) for x in inputs[1:]]
         + [
             pltpu.VMEM((count, LANES), I32),
+            pltpu.VMEM((count, FACET), F32),
+            pltpu.VMEM((count, FACET), F32),
             pltpu.VMEM((16 * count, FACET), BF16),
-            pltpu.SemaphoreType.DMA((6,)),
+            pltpu.SemaphoreType.DMA((8,)),
         ],
         far,
         count=count,
         cap=cap,
     )
+    near = [
+        lax.ppermute(corner, "freq", [(g, (g + k) % groups) for g in range(groups)])
+        for k in range(1, groups)
+    ]
     got = exchange(send, "facet", count)
     columns, kern_u, kern_h, vis, spread, own = call(
         first_kernel,
         (
             shape(height, LANES),
-            shape(SUB, slots),
+            shape(2 * SUB, slots, dtype=BF16),
             shape(2 * height, slots),
             shape(8, slots),
             shape(total * height, LANES),
@@ -429,12 +466,18 @@
         scale=scale,
     )
     everyone = exchange(spread, ("freq", "facet"), total)
-    phases = call(
-        phase_kernel,
-        (shape(total, FACET), shape(total, FACET), shape(total, LANES), shape(total, LANES)),
+    *phases, select = call(
+        prepare_kernel,
+        (
+            shape(total, FACET),
+            shape(total, FACET),
+            shape(total, LANES),
+            shape(total, LANES),
+            shape(total * LANES, LANES, dtype=BF16),
+        ),
         [corner, *near],
         [],
-        "phases",
+        "prepare",
         [pltpu.VMEM((total, LANES), I32)],
         count=count,
         groups=groups,
@@ -442,10 +485,9 @@
     back = call(
         second_kernel,
         shape(total * BACK, LANES),
-        [corner, *near],
-        [everyone, own, columns, kern_u, kern_h, vis],
+        [],
+        [everyone, select, own, columns, kern_u, kern_h, vis],
         "second_cycle",
-        [pltpu.VMEM((height, LANES), F32)],
         count=count,
         cap=cap,
         groups=groups,

time: 51.7 us -> 47.6 us (0.921)
  blocking collectives: 16.4 us -> 27.2 us
  waiting for transfers between devices: 16.1 us -> 6.75 us
  starting transfers between devices: 7.35 us -> 4.42 us
  Pallas kernels: 10.2 us -> 8.25 us
  local copies, waits for them, and re-layouts: 0.68 us -> 0.01 us
    all_to_all x1 -> x2, blocking collectives: 16.4 us -> 27.2 us  [exchange(): lax.all_to_all(view, axes, split_axis=0, concat_axis=0, tiled=True)]
    all_to_all x2 -> x1, waiting for transfers between devices: 14.1 us -> 4.78 us  [exchange(): lax.all_to_all(view, axes, split_axis=0, concat_axis=0, tiled=True)]
    all_to_all x2 -> x1, starting transfers between devices: 5.53 us -> 2.6 us  [exchange(): lax.all_to_all(view, axes, split_axis=0, concat_axis=0, tiled=True)]
    pallas_call x5, Pallas kernels: 10.2 us -> 8.25 us  [call(): pl.pallas_call(lambda *refs: body(*refs, **sizes), out_shape=out_shape, i...]
    unnamed x4 -> x2, local copies, waits for them, and re-layouts: 0.68 us -> 0.01 us
  transfers between devices with their start and end apart: 3 -> 2, of which waited for: 3 -> 2; matrix products, arithmetic and copies ran while one was open for 0% -> 0% of each run, Pallas kernels for 1% -> 4%
where the time goes in v3:
time: 47.6 us; the launch traced here: 47.3 us
  blocking collectives  27.2 us (57%)
  Pallas kernels  8.25 us (17%)
  waiting for transfers between devices  6.75 us (14%)
  starting transfers between devices  4.42 us (9%)
  between operations  0.68 us (1%)
    all_to_all x2, blocking collectives, exchange(): lax.all_to_all(view, axes, split_axis=0, concat_axis=0, tiled=True)  27.2 us
    pallas_call x5, Pallas kernels, call(): pl.pallas_call(lambda *refs: body(*refs, **sizes), out_shape=out_shape, i...  8.25 us
    all_to_all x1, waiting for transfers between devices, exchange(): lax.all_to_all(view, axes, split_axis=0, concat_axis=0, tiled=True)  4.78 us
    all_to_all x1, starting transfers between devices, exchange(): lax.all_to_all(view, axes, split_axis=0, concat_axis=0, tiled=True)  2.6 us
    ppermute x1, waiting for transfers between devices, on_device(): lax.ppermute(corner, 'freq', [(g, (g + k) % groups) for g in range(groups)])  1.97 us
    ppermute x1, starting transfers between devices, on_device(): lax.ppermute(corner, 'freq', [(g, (g + k) % groups) for g in range(groups)])  1.83 us
  transfers between devices with their start and end apart: 2, of which 2 were waited for; matrix products, arithmetic and copies ran while one was open for 0% of the time, Pallas kernels for 4%

profile of v3, /device:TPU:0, one launch (start us, length us, event | category | flops | bytes accessed | tf_op | source)
XLA Modules:
  0.0 47.3 jit_solution(9751813858856526797)
XLA Ops:
  0.6 2.3 %send_rows.1 = (f32[416,128]{1,0:T(8,128)S(1)}, bf16[128,2048]{1,0:T(8,128)(2,1)S(1)}, f32[16,256]{1,0:T(8,128)S(1)}, s32[1,256]{1,0:T(1,128)S(1)}, s32[2,16]{1,0:T(2,128)S(1)}) custom-call(s32[2,16]{1,0:T(2,128)} %bitcast.15, s32[1,256]{1,0:T(1,128)} %bitcast.16, f32[2,256]{1,0:T(2,128)} %refs_2_.1, f32[16,256]{1,0:T(8,128)} %refs_3_.1, f32[16,256]{1,0:T(8,128)} %refs_4_.1, ...), custom_call_target="tpu_custom_call" | custom-call | tf_op jit(solution)/shard_map/send_rows/pallas_call | solution.py:405
  3.0 16.4 %all_to_all.15 = f32[16,1,3328]{2,1,0:T(1,128)S(1)} all-to-all(f32[16,1,3328]{2,1,0:T(1,128)S(1)} %bitcast.14), channel_id=1, replica_groups=mesh['freq'=2,'facet'=16] {'facet'}, dimensions={0} | all-to-all | bytes 425984 | tf_op jit(solution)/shard_map/all_to_all | solution.py:417
  19.4 2.0 %first_cycle.1 = (f32[16,128]{1,0:T(8,128)S(1)}, bf16[128,1024]{1,0:T(8,128)(2,1)S(1)}, f32[32,1024]{1,0:T(8,128)S(1)}, f32[8,1024]{1,0:T(8,128)S(1)}, f32[512,128]{1,0:T(8,128)}, /*index=5*/f32[16,128]{1,0:T(8,128)S(1)}) custom-call(s32[2,16]{1,0:T(2,128)S(1)} %get-tuple-element.18.refs_0_, f32[416,128]{1,0:T(8,128)S(1)} %bitcast.11), custom_call_target="tpu_custom_call" | custom-call | tf_op jit(solution)/shard_map/first_cycle/pallas_call | solution.py:405
  21.4 2.6 %all-to-all-start.1 = ((f32[32,1,2048]{2,1,0:T(1,128)}), f32[32,1,2048]{2,1,0:T(1,128)S(1)}, u32[]{:S(2)}, u32[]{:S(2)}) async-start(f32[32,1,2048]{2,1,0:T(1,128)} %bitcast.5), calls=%async_computation.1 | async-start | bytes 524288 | tf_op jit(solution)/shard_map/all_to_all | solution.py:417
  24.0 1.8 %collective-permute-start = (s32[2,16]{1,0:T(2,128)S(1)}, s32[2,16]{1,0:T(2,128)S(1)}, u32[]{:S(2)}, u32[]{:S(2)}) collective-permute-start(s32[2,16]{1,0:T(2,128)S(1)} %get-tuple-element.18.refs_0_), channel_id=1, source_target_pairs={{0,16},{16,0},{1,17},{17,1},{2,18},{18,2},{3,19},{19,3},{4,20},{20... | collective-permute-start | bytes 392 | tf_op jit(solution)/shard_map/ppermute | solution.py:446
  25.8 2.0 %collective-permute-done.refs_1_ = s32[2,16]{1,0:T(2,128)S(1)} collective-permute-done((s32[2,16]{1,0:T(2,128)S(1)}, s32[2,16]{1,0:T(2,128)S(1)}, u32[]{:S(2)}, u32[]{:S(2)}) %collective-permute-start) | collective-permute-done | bytes 160 | tf_op jit(solution)/shard_map/ppermute | solution.py:446
  27.8 1.7 %prepare.1 = (f32[32,2048]{1,0:T(8,128)S(1)}, f32[32,2048]{1,0:T(8,128)S(1)}, f32[32,128]{1,0:T(8,128)S(1)}, f32[32,128]{1,0:T(8,128)S(1)}, bf16[4096,128]{1,0:T(8,128)(2,1)S(1)}) custom-call(s32[2,16]{1,0:T(2,128)S(1)} %get-tuple-element.18.refs_0_, s32[2,16]{1,0:T(2,128)S(1)} %collective-permute-done.refs_1_), custom_call_target="tpu_custom_call" | custom-call | tf_op jit(solution)/shard_map/prepare/pallas_call | solution.py:405
  29.4 4.8 %all-to-all-done.1 = f32[32,1,2048]{2,1,0:T(1,128)S(1)} async-done(((f32[32,1,2048]{2,1,0:T(1,128)}), f32[32,1,2048]{2,1,0:T(1,128)S(1)}, u32[]{:S(2)}, u32[]{:S(2)}) %all-to-all-start.1) | async-done | bytes 262176 | tf_op jit(solution)/shard_map/all_to_all | solution.py:417
  34.2 0.8 %second_cycle.1 = f32[288,128]{1,0:T(8,128)S(1)} custom-call(f32[512,128]{1,0:T(8,128)S(1)} %bitcast.10, bf16[4096,128]{1,0:T(8,128)(2,1)S(1)} %get-tuple-element.21.refs_1_, f32[16,128]{1,0:T(8,128)S(1)} %get-tuple-element.22.refs_2_, f32[16,128]{1,0:T(8,128)S(1)} %get-tuple-element.23.refs_3_, bf16[128,1024]{1,0:T(8,128)(2,1)S(1)} %get-tuple-element.24.refs_4_, ...), custom_call_target="tpu_custom_call" | custom-call | tf_op jit(solution)/shard_map/second_cycle/pallas_call | solution.py:405
  35.0 0.0 copy-start
  35.0 10.8 %all_to_all.16 = f32[32,1,1152]{2,1,0:T(1,128)S(1)} all-to-all(f32[32,1,1152]{2,1,0:T(1,128)S(1)} %bitcast.13), channel_id=1, replica_groups=mesh['freq'=2,'facet'=16] {'freq','facet'}, dimensions={0} | all-to-all | bytes 294912 | tf_op jit(solution)/shard_map/all_to_all | solution.py:417
  45.8 0.0 copy-done
  45.8 1.5 %form_image.1 = (f32[8,2048]{1,0:T(8,128)}, f32[2,256]{1,0:T(2,128)}) custom-call(f32[288,128]{1,0:T(8,128)S(1)} %bitcast.12, bf16[128,2048]{1,0:T(8,128)(2,1)S(1)} %get-tuple-element.27.refs_1_, f32[32,2048]{1,0:T(8,128)S(1)} %get-tuple-element.28.refs_2_, f32[32,2048]{1,0:T(8,128)S(1)} %get-tuple-element.29.refs_3_, ...), custom_call_target="tpu_custom_call" | custom-call | tf_op jit(solution)/shard_map/form_image/pallas_call | solution.py:405
Async XLA Ops:
  21.4 12.9 %all-to-all-start.1 = ((f32[32,1,2048]{2,1,0:T(1,128)}), f32[32,1,2048]{2,1,0:T(1,128)S(1)}, u32[]{:S(2)}, u32[]{:S(2)}) async-start(f32[32,1,2048]{2,1,0:T(1,128)} %bitcast.5), calls=%async_computation.1 | async-start | bytes 524288 | tf_op jit(solution)/shard_map/all_to_all | solution.py:417
  24.0 3.8 %collective-permute-start = (s32[2,16]{1,0:T(2,128)S(1)}, s32[2,16]{1,0:T(2,128)S(1)}, u32[]{:S(2)}, u32[]{:S(2)}) collective-permute-start(s32[2,16]{1,0:T(2,128)S(1)} %get-tuple-element.18.refs_0_), channel_id=1, source_target_pairs={{0,16},{16,0},{1,17},{17,1},{2,18},{18,2},{3,19},{19,3},{4,20},{20... | collective-permute-start | bytes 392 | tf_op jit(solution)/shard_map/ppermute | solution.py:446
  35.0 10.8 %copy-start = (f32[8,2048]{1,0:T(8,128)S(1)}, f32[8,2048]{1,0:T(8,128)}, u32[]{:S(2)}) copy-start(f32[8,2048]{1,0:T(8,128)} %refs_8_.1) | copy-start | bytes 196612

commit v4 on v3

--- a/solution.py
+++ b/solution.py
@@ -14,8 +14,9 @@
 SUPPORT = 16
 LANES = 128
 ACROSS = GRID // FACET
-GROUPS = 6
+GROUPS = 4
 BACK = FROWS + 1
+CHUNK = 512
 GAIN_STEP = 0.5
 
 F32 = jnp.float32
@@ -43,16 +44,12 @@
     return cos_v, sin_v
 
 
-def phase_rows(freq):
+def phase_tiles(freq):
     cos_v, sin_v = phase_pair(freq * iota(freq.shape, 1))
     turn_c, turn_s = phase_pair(freq * LANES)
-    cos_l, sin_l = [cos_v], [sin_v]
-    while len(cos_l) < FACET // LANES:
-        more_c = [c * turn_c - s * turn_s for c, s in zip(cos_l, sin_l)]
-        more_s = [s * turn_c + c * turn_s for c, s in zip(cos_l, sin_l)]
-        cos_l, sin_l = cos_l + more_c, sin_l + more_s
-        turn_c, turn_s = turn_c * turn_c - turn_s * turn_s, 2.0 * turn_c * turn_s
-    return jnp.concatenate(cos_l, axis=1), jnp.concatenate(sin_l, axis=1)
+    for tile in range(FACET // LANES):
+        yield tile * LANES, cos_v, sin_v
+        cos_v, sin_v = cos_v * turn_c - sin_v * turn_s, sin_v * turn_c + cos_v * turn_s
 
 
 def dot_nt(left, right, precision=None):
@@ -83,14 +80,13 @@
 
 def layout_of(cap):
     lane_groups = LANES // cap
-    row_blocks = -(-GROUPS // lane_groups)
-    rows = 8 * row_blocks - (6 if row_blocks == 3 else 0)
-    return lane_groups, row_blocks, FROWS + rows
-
-
-def read_block(ref, start, rows):
-    block = ref[start : start + rows, :]
-    return block if rows == 8 else jnp.concatenate([block, jnp.zeros((8 - rows, LANES), F32)], axis=0)
+    row_blocks = -(-GROUPS // min(lane_groups, GROUPS))
+    return lane_groups, row_blocks, FROWS + 8 * row_blocks + 2
+
+
+def turn(value, shift):
+    shift = shift % LANES
+    return pltpu.roll(value, shift, 1) if shift else value
 
 
 def slot_parts(owner_row, count):
@@ -103,7 +99,7 @@
 
 def send_kernel(
     corner_hbm, owner_hbm, vis_hbm, ku_hbm, kv_hbm, off_hbm, image_hbm,
-    send_ref, table_ref, hits_ref, rank_ref, corner_out,
+    send_ref, table_ref, hits_ref, rank_ref, corner_out, start_ref,
     corner_ref, owner_ref, vis_ref, ku_ref, kv_ref, off_ref, image_ref,
     freq_ref, cos_ref, sin_ref, mod_ref, sem_ref, *, count, cap,
 ):
@@ -117,21 +113,24 @@
         copy.start()
     facet = lax.axis_index("facet")
     x_start = facet % ACROSS * FACET - GRID // 2
-    cos_t, sin_t = phase_rows(iota((SUB, LANES), 0))
-    table = jnp.concatenate([cos_t, sin_t], axis=0).astype(BF16)
-    table_ref[...] = table
+    for at, cos_t, sin_t in phase_tiles(iota((SUB, LANES), 0)):
+        table_ref[:SUB, at : at + LANES] = cos_t.astype(BF16)
+        table_ref[SUB:, at : at + LANES] = sin_t.astype(BF16)
     copies[0].wait()
+    start_ref[...] = jnp.full(start_ref.shape, corner_ref[1, facet], I32)
     for s in range(count):
         freq_ref[s : s + 1, :] = jnp.full((1, LANES), corner_ref[0, s], I32)
     freq = freq_ref[...]
-    cos_ref[...], sin_ref[...] = phase_rows(freq)
+    for at, cos_u, sin_u in phase_tiles(freq):
+        cos_ref[:, at : at + LANES] = cos_u
+        sin_ref[:, at : at + LANES] = -sin_u
     for copy in copies[1:]:
         copy.wait()
     image = image_ref[...]
     for s in range(count):
-        both = jnp.concatenate([image * spread_row(cos_ref, s), -image * spread_row(sin_ref, s)], axis=0)
+        both = jnp.concatenate([image * spread_row(cos_ref, s), image * spread_row(sin_ref, s)], axis=0)
         mod_ref[16 * s : 16 * s + 16, :] = both.astype(BF16)
-    prod = dot_nt(mod_ref[...], table)
+    prod = dot_nt(mod_ref[...], table_ref[...])
     lane = iota((FROWS, LANES), 1)
     low = lane < SUB
     cos_x, sin_x = phase_pair((freq + (iota(freq.shape, 1) & (SUB - 1))) * x_start)
@@ -149,29 +148,36 @@
     hits, rank = slot_parts(owner_row, count)
     hits_ref[...] = hits
     rank_ref[...] = rank
-    blank = jnp.zeros((6, rows), F32)
-    vis = jnp.concatenate([vis_ref[...], blank], axis=0)
-    offset = jnp.concatenate([off_ref[...].astype(F32), blank], axis=0)
-    parts = [ku_ref[0:8, :], ku_ref[8:16, :], vis, kv_ref[0:8, :], kv_ref[8:16, :], offset]
-    parts = parts + [jnp.zeros((8, rows), F32)] * (-len(parts) % row_blocks)
-    groups = len(parts) // row_blocks
+    place = [
+        (iota((LANES, rows), 0) == rank + group * cap).astype(F32).astype(BF16)
+        for group in range(max(2, GROUPS // row_blocks))
+    ]
     high = 16 * -(-row_blocks // 2)
+    taps = jnp.concatenate([ku_ref[...], kv_ref[...]], axis=0)
     left, places = [], []
-    for group in range(groups):
-        mine = parts[group * row_blocks : (group + 1) * row_blocks]
-        mine = mine + [jnp.zeros((8, rows), F32)] * (high // 8 - row_blocks)
-        both = split(jnp.concatenate(mine, axis=0))
-        place = (iota((LANES, rows), 0) == rank + group * cap).astype(F32).astype(BF16)
+    for group in range(GROUPS // row_blocks):
+        mine = taps[8 * row_blocks * group : 8 * row_blocks * (group + 1)]
+        if high > 8 * row_blocks:
+            mine = jnp.concatenate([mine, jnp.zeros((high - 8 * row_blocks, rows), F32)], axis=0)
+        both = split(mine)
         left += [both[:high], both[high:]]
-        places += [place, place]
+        places += [place[group], place[group]]
     stacked = jnp.concatenate(left, axis=1)
-    wide = jnp.concatenate([hits] * (2 * groups), axis=1)
+    half_hits = jnp.concatenate([hits] * len(left), axis=1)
     masked = [
-        stacked * jnp.broadcast_to(wide[s : s + 1], stacked.shape).astype(BF16) for s in range(count)
+        stacked * jnp.broadcast_to(half_hits[s : s + 1], stacked.shape).astype(BF16) for s in range(count)
     ]
     total = dot_nt(jnp.concatenate(masked, axis=0), jnp.concatenate(places, axis=1))
+    vis, offset = vis_ref[...], off_ref[...].astype(F32)
+    vis = split(jnp.concatenate([hits * vis[0:1], hits * vis[1:2]], axis=0))
+    offset = jnp.concatenate([hits * offset[0:1], hits * offset[1:2]], axis=0).astype(BF16)
+    misc = jnp.concatenate([vis[: 2 * count], vis[2 * count :], offset], axis=1)
+    misc = dot_nt(misc, jnp.concatenate([place[0], place[0], place[1]], axis=1))
     for s in range(count):
-        send_ref[piece * s + FROWS : piece * (s + 1), :] = total[high * s : high * s + piece - FROWS]
+        at = piece * (s + 1) - 2
+        send_ref[piece * s + FROWS : at, :] = total[high * s : high * s + 8 * row_blocks]
+        send_ref[at : at + 1, :] = misc[s : s + 1]
+        send_ref[at + 1 : at + 2, :] = misc[count + s : count + s + 1]
 
 
 def place_kernel(taps, offset):
@@ -212,11 +218,10 @@
 
 
 def first_kernel(
-    corner_ref, got_ref, col_ref, ku_ref, kh_ref, vis_ref, rows_ref, own_ref, *, count, cap, groups, scale,
+    start_ref, got_ref, col_ref, ku_ref, kh_ref, vis_ref, rows_ref, own_ref, *, count, cap, groups, scale,
 ):
     lane_groups, row_blocks, piece = layout_of(cap)
     height = count // ACROSS * FROWS
-    v_start = corner_ref[1, lax.axis_index("facet")]
     sums = []
     for down in range(count // ACROSS):
         total = got_ref[piece * down * ACROSS : piece * down * ACROSS + FROWS, :]
@@ -229,28 +234,28 @@
     lane_group = iota((8, LANES), 1) // cap
     u_list, v_list, vis_list = [], [], []
     for tile in range(count // lane_groups):
-        found = []
-        for k in range(GROUPS):
-            block, group = k % row_blocks, k // row_blocks
-            value = None
-            for j in range(lane_groups):
-                at = FROWS + 8 * block
-                moved = read_block(got_ref, piece * (tile * lane_groups + j) + at, min(8, piece - at))
-                shift = (j - group) * cap % LANES
-                if shift:
-                    moved = pltpu.roll(moved, shift, 1)
-                value = moved if value is None else jnp.where(lane_group == j, moved, value)
-            found.append(value)
+        found = [None] * (GROUPS + 2)
+        for j in range(lane_groups):
+            base = piece * (tile * lane_groups + j)
+            moved = []
+            for k in range(GROUPS):
+                at = base + FROWS + 8 * (k % row_blocks)
+                moved.append(turn(got_ref[at : at + 8, :], (j - k // row_blocks) * cap))
+            misc = got_ref[base + piece - 2 : base + piece, :]
+            moved += [turn(misc, j * cap), turn(misc, (j - 1) * cap)]
+            for k, value in enumerate(moved):
+                mine = lane_group[: value.shape[0]] == j
+                found[k] = value if j == 0 else jnp.where(mine, value, found[k])
         offset = found[5].astype(I32)
         u_list.append(place_kernel(jnp.concatenate(found[0:2], axis=0), offset[0:1]))
-        v_list.append(place_kernel(jnp.concatenate(found[3:5], axis=0), offset[1:2]))
-        vis_list.append(found[2])
+        v_list.append(place_kernel(jnp.concatenate(found[2:4], axis=0), offset[1:2]))
+        vis_list.append(found[4])
     kern_u = jnp.concatenate(u_list, axis=1)
     kern_v = jnp.concatenate(v_list, axis=1)
     vis = jnp.concatenate(vis_list, axis=1)
     row = iota((height, LANES), 0)
     y_pos = row // FROWS * FACET - GRID // 2 + row % FROWS
-    cos_y, sin_y = phase_pair((v_start + (iota((height, LANES), 1) & (SUB - 1))) * y_pos)
+    cos_y, sin_y = phase_pair((start_ref[0:1, :] + (iota((height, LANES), 1) & (SUB - 1))) * y_pos)
     kern_h = fold(dot_nn(split(jnp.concatenate([cos_y, -sin_y], axis=0)), split(kern_v)))
     kern_u = split(kern_u)
     ku_ref[...] = kern_u
@@ -270,11 +275,6 @@
     for k in range(1, groups):
         value = jnp.where(back == k, refs[k][0, index], value)
     return value
-
-
-def turn(value, shift):
-    shift = shift % LANES
-    return pltpu.roll(value, shift, 1) if shift else value
 
 
 def second_kernel(
@@ -345,29 +345,34 @@
     cos_x, sin_x = phase_pair((freq + (iota(freq.shape, 1) & (SUB - 1))) * x_start)
     cos_x_ref[...] = cos_x
     sin_x_ref[...] = jnp.where(iota(freq.shape, 1) < SUB, -sin_x, sin_x)
-    cos_ref[...], sin_ref[...] = phase_rows(freq)
+    total = groups * count
+    for at, cos_u, sin_u in phase_tiles(freq):
+        place = slice(at // CHUNK * total, (at // CHUNK + 1) * total), slice(at % CHUNK, at % CHUNK + LANES)
+        cos_ref[place] = cos_u
+        sin_ref[place] = -sin_u
 
 
 def image_kernel(
     got_ref, table_ref, cos_ref, sin_ref, cos_x_ref, sin_x_ref, hits_ref, rank_ref, image_ref,
-    out_ref, res_ref, *, count, groups, cap, scale,
+    out_ref, res_ref, left_ref, *, count, groups, cap, scale,
 ):
     total = groups * count
     low = iota((FROWS, LANES), 1) < SUB
     cos_x, sin_x = cos_x_ref[...], sin_x_ref[...]
-    left = []
     for d in range(total):
         block = got_ref[BACK * d : BACK * d + 8, :]
         moved = block * cos_x[d : d + 1] + pltpu.roll(block, SUB, 1) * sin_x[d : d + 1]
-        left.append(jnp.where(low, moved, -moved))
-        left.append(pltpu.roll(moved, SUB, 1))
-    left = jnp.concatenate(left, axis=0).astype(BF16)
-    both = dot_nn(left, table_ref[...])
-    dirty = jnp.zeros((FROWS, FACET), F32)
-    for d in range(total):
-        dirty = dirty + both[16 * d : 16 * d + 8] * spread_row(cos_ref, d)
-        dirty = dirty - both[16 * d + 8 : 16 * d + 16] * spread_row(sin_ref, d)
-    out_ref[...] = image_ref[...] + (GAIN_STEP * scale) * dirty
+        both = jnp.concatenate([jnp.where(low, moved, -moved), pltpu.roll(moved, SUB, 1)], axis=0)
+        left_ref[16 * d : 16 * d + 16, :] = both.astype(BF16)
+    for at in range(0, FACET, CHUNK):
+        cut = slice(at, at + CHUNK)
+        both = dot_nn(left_ref[...], table_ref[:, cut])
+        dirty = jnp.zeros((FROWS, CHUNK), F32)
+        for d in range(total):
+            row = at // CHUNK * total + d
+            dirty = dirty + both[16 * d : 16 * d + 8] * spread_row(cos_ref, row)
+            dirty = dirty + both[16 * d + 8 : 16 * d + 16] * spread_row(sin_ref, row)
+        out_ref[:, cut] = image_ref[:, cut] + (GAIN_STEP * scale) * dirty
 
     rows = rank_ref.shape[1]
     first = lax.axis_index("freq") * (count * BACK) + 8
@@ -417,7 +422,7 @@
         return lax.all_to_all(view, axes, split_axis=0, concat_axis=0, tiled=True).reshape(block.shape)
 
     inputs = [corner, owner_row, visibilities, kernel_u, kernel_v, offsets, model_image]
-    send, table, hits, rank, corner = call(
+    send, table, hits, rank, corner, start = call(
         send_kernel,
         (
             shape(count * piece, LANES),
@@ -425,6 +430,7 @@
             shape(count, rows),
             shape(1, rows, dtype=I32),
             shape(*corner.shape, dtype=I32),
+            shape(8, LANES, dtype=I32),
         ),
         [],
         [pltpu.with_memory_space_constraint(x, pltpu.HBM) for x in inputs],
@@ -453,12 +459,12 @@
             shape(height, LANES),
             shape(2 * SUB, slots, dtype=BF16),
             shape(2 * height, slots),
-            shape(8, slots),
+            shape(2, slots),
             shape(total * height, LANES),
             shape(height, LANES),
         ),
-        [corner],
-        [got],
+        [],
+        [start, got],
         "first_cycle",
         count=count,
         cap=cap,
@@ -469,8 +475,8 @@
     *phases, select = call(
         prepare_kernel,
         (
-            shape(total, FACET),
-            shape(total, FACET),
+            shape(FACET // CHUNK * total, CHUNK),
+            shape(FACET // CHUNK * total, CHUNK),
             shape(total, LANES),
             shape(total, LANES),
             shape(total * LANES, LANES, dtype=BF16),
@@ -500,6 +506,7 @@
         [],
         [returned, table, *phases, hits, rank, model_image],
         "form_image",
+        [pltpu.VMEM((16 * total, LANES), BF16)],
         count=count,
         groups=groups,
         cap=cap,

time: 47.6 us -> 46.5 us (0.977)
  Pallas kernels: 8.25 us -> 7.12 us
    pallas_call x5, Pallas kernels: 8.25 us -> 7.12 us  [call(): pl.pallas_call(lambda *refs: body(*refs, **sizes), out_shape=out_shape, i...]
where the time goes in v4:
time: 46.5 us; the launch traced here: 46.2 us
  blocking collectives  27.2 us (58%)
  Pallas kernels  7.12 us (15%)
  waiting for transfers between devices  6.75 us (15%)
  starting transfers between devices  4.43 us (10%)
  between operations  0.68 us (1%)
    all_to_all x2, blocking collectives, exchange(): lax.all_to_all(view, axes, split_axis=0, concat_axis=0, tiled=True)  27.2 us
    pallas_call x5, Pallas kernels, call(): pl.pallas_call(lambda *refs: body(*refs, **sizes), out_shape=out_shape, i...  7.12 us
    all_to_all x1, waiting for transfers between devices, exchange(): lax.all_to_all(view, axes, split_axis=0, concat_axis=0, tiled=True)  4.77 us
    all_to_all x1, starting transfers between devices, exchange(): lax.all_to_all(view, axes, split_axis=0, concat_axis=0, tiled=True)  2.6 us
    ppermute x1, waiting for transfers between devices, on_device(): lax.ppermute(corner, 'freq', [(g, (g + k) % groups) for g in range(groups)])  1.97 us
    ppermute x1, starting transfers between devices, on_device(): lax.ppermute(corner, 'freq', [(g, (g + k) % groups) for g in range(groups)])  1.83 us
  transfers between devices with their start and end apart: 2, of which 2 were waited for; matrix products, arithmetic and copies ran while one was open for 0% of the time, Pallas kernels for 4%

profile of v4, /device:TPU:0, one launch (start us, length us, event | category | flops | bytes accessed | tf_op | source)
XLA Modules:
  0.0 46.2 jit_solution(4390610325087328361)
XLA Ops:
  0.6 1.7 %send_rows.1 = (f32[416,128]{1,0:T(8,128)S(1)}, bf16[128,2048]{1,0:T(8,128)(2,1)S(1)}, f32[16,256]{1,0:T(8,128)S(1)}, s32[1,256]{1,0:T(1,128)S(1)}, s32[2,16]{1,0:T(2,128)S(1)}, /*index=5*/s32[8,128]{1,0:T(8,128)S(1)}) custom-call(s32[2,16]{1,0:T(2,128)} %bitcast.15, s32[1,256]{1,0:T(1,128)} %bitcast.16, f32[2,256]{1,0:T(2,128)} %refs_2_.1, ...), custom_call_target="tpu_custom_call" | custom-call | tf_op jit(solution)/shard_map/send_rows/pallas_call | solution.py:410
  2.3 16.4 %all_to_all.15 = f32[16,1,3328]{2,1,0:T(1,128)S(1)} all-to-all(f32[16,1,3328]{2,1,0:T(1,128)S(1)} %bitcast.14), channel_id=1, replica_groups=mesh['freq'=2,'facet'=16] {'facet'}, dimensions={0} | all-to-all | bytes 425984 | tf_op jit(solution)/shard_map/all_to_all | solution.py:422
  18.8 1.4 %first_cycle.1 = (f32[16,128]{1,0:T(8,128)S(1)}, bf16[128,1024]{1,0:T(8,128)(2,1)S(1)}, f32[32,1024]{1,0:T(8,128)S(1)}, f32[2,1024]{1,0:T(2,128)S(1)}, f32[512,128]{1,0:T(8,128)}, /*index=5*/f32[16,128]{1,0:T(8,128)S(1)}) custom-call(s32[8,128]{1,0:T(8,128)S(1)} %get-tuple-element.19.refs_0_, f32[416,128]{1,0:T(8,128)S(1)} %bitcast.11), custom_call_target="tpu_custom_call" | custom-call | tf_op jit(solution)/shard_map/first_cycle/pallas_call | solution.py:410
  20.2 2.6 %all-to-all-start.1 = ((f32[32,1,2048]{2,1,0:T(1,128)}), f32[32,1,2048]{2,1,0:T(1,128)S(1)}, u32[]{:S(2)}, u32[]{:S(2)}) async-start(f32[32,1,2048]{2,1,0:T(1,128)} %bitcast.5), calls=%async_computation.1 | async-start | bytes 524288 | tf_op jit(solution)/shard_map/all_to_all | solution.py:422
  22.8 1.8 %collective-permute-start = (s32[2,16]{1,0:T(2,128)S(1)}, s32[2,16]{1,0:T(2,128)S(1)}, u32[]{:S(2)}, u32[]{:S(2)}) collective-permute-start(s32[2,16]{1,0:T(2,128)S(1)} %get-tuple-element.22.refs_0_), channel_id=1, source_target_pairs={{0,16},{16,0},{1,17},{17,1},{2,18},{18,2},{3,19},{19,3},{4,20},{20... | collective-permute-start | bytes 392 | tf_op jit(solution)/shard_map/ppermute | solution.py:452
  24.6 2.0 %collective-permute-done.refs_1_ = s32[2,16]{1,0:T(2,128)S(1)} collective-permute-done((s32[2,16]{1,0:T(2,128)S(1)}, s32[2,16]{1,0:T(2,128)S(1)}, u32[]{:S(2)}, u32[]{:S(2)}) %collective-permute-start) | collective-permute-done | bytes 160 | tf_op jit(solution)/shard_map/ppermute | solution.py:452
  26.6 1.7 %prepare.1 = (f32[128,512]{1,0:T(8,128)S(1)}, f32[128,512]{1,0:T(8,128)S(1)}, f32[32,128]{1,0:T(8,128)S(1)}, f32[32,128]{1,0:T(8,128)S(1)}, bf16[4096,128]{1,0:T(8,128)(2,1)S(1)}) custom-call(s32[2,16]{1,0:T(2,128)S(1)} %get-tuple-element.22.refs_0_, s32[2,16]{1,0:T(2,128)S(1)} %collective-permute-done.refs_1_), custom_call_target="tpu_custom_call" | custom-call | tf_op jit(solution)/shard_map/prepare/pallas_call | solution.py:410
  28.3 4.8 %all-to-all-done.1 = f32[32,1,2048]{2,1,0:T(1,128)S(1)} async-done(((f32[32,1,2048]{2,1,0:T(1,128)}), f32[32,1,2048]{2,1,0:T(1,128)S(1)}, u32[]{:S(2)}, u32[]{:S(2)}) %all-to-all-start.1) | async-done | bytes 262176 | tf_op jit(solution)/shard_map/all_to_all | solution.py:422
  33.1 0.8 %second_cycle.1 = f32[288,128]{1,0:T(8,128)S(1)} custom-call(f32[512,128]{1,0:T(8,128)S(1)} %bitcast.10, bf16[4096,128]{1,0:T(8,128)(2,1)S(1)} %get-tuple-element.23.refs_1_, f32[16,128]{1,0:T(8,128)S(1)} %get-tuple-element.24.refs_2_, f32[16,128]{1,0:T(8,128)S(1)} %get-tuple-element.25.refs_3_, bf16[128,1024]{1,0:T(8,128)(2,1)S(1)} %get-tuple-element.26.refs_4_, ...), custom_call_target="tpu_custom_call" | custom-call | tf_op jit(solution)/shard_map/second_cycle/pallas_call | solution.py:410
  33.9 0.0 copy-start
  33.9 10.8 %all_to_all.16 = f32[32,1,1152]{2,1,0:T(1,128)S(1)} all-to-all(f32[32,1,1152]{2,1,0:T(1,128)S(1)} %bitcast.13), channel_id=1, replica_groups=mesh['freq'=2,'facet'=16] {'freq','facet'}, dimensions={0} | all-to-all | bytes 294912 | tf_op jit(solution)/shard_map/all_to_all | solution.py:422
  44.6 0.0 copy-done
  44.6 1.5 %form_image.1 = (f32[8,2048]{1,0:T(8,128)}, f32[2,256]{1,0:T(2,128)}) custom-call(f32[288,128]{1,0:T(8,128)S(1)} %bitcast.12, bf16[128,2048]{1,0:T(8,128)(2,1)S(1)} %get-tuple-element.29.refs_1_, f32[128,512]{1,0:T(8,128)S(1)} %get-tuple-element.30.refs_2_, f32[128,512]{1,0:T(8,128)S(1)} %get-tuple-element.31.refs_3_, ...), custom_call_target="tpu_custom_call" | custom-call | tf_op jit(solution)/shard_map/form_image/pallas_call | solution.py:410
Async XLA Ops:
  20.2 12.9 %all-to-all-start.1 = ((f32[32,1,2048]{2,1,0:T(1,128)}), f32[32,1,2048]{2,1,0:T(1,128)S(1)}, u32[]{:S(2)}, u32[]{:S(2)}) async-start(f32[32,1,2048]{2,1,0:T(1,128)} %bitcast.5), calls=%async_computation.1 | async-start | bytes 524288 | tf_op jit(solution)/shard_map/all_to_all | solution.py:422
  22.8 3.8 %collective-permute-start = (s32[2,16]{1,0:T(2,128)S(1)}, s32[2,16]{1,0:T(2,128)S(1)}, u32[]{:S(2)}, u32[]{:S(2)}) collective-permute-start(s32[2,16]{1,0:T(2,128)S(1)} %get-tuple-element.22.refs_0_), channel_id=1, source_target_pairs={{0,16},{16,0},{1,17},{17,1},{2,18},{18,2},{3,19},{19,3},{4,20},{20... | collective-permute-start | bytes 392 | tf_op jit(solution)/shard_map/ppermute | solution.py:452
  33.9 10.8 %copy-start = (f32[8,2048]{1,0:T(8,128)S(1)}, f32[8,2048]{1,0:T(8,128)}, u32[]{:S(2)}) copy-start(f32[8,2048]{1,0:T(8,128)} %refs_8_.1) | copy-start | bytes 196612

commit v5 on v4

--- a/solution.py
+++ b/solution.py
@@ -16,7 +16,7 @@
 ACROSS = GRID // FACET
 GROUPS = 4
 BACK = FROWS + 1
-CHUNK = 512
+TURNS = FACET // LANES
 GAIN_STEP = 0.5
 
 F32 = jnp.float32
@@ -89,6 +89,14 @@
     return pltpu.roll(value, shift, 1) if shift else value
 
 
+def side_by_side(ref, height, half=None):
+    starts = list(range(0, ref.shape[0], height))
+    if half is not None:
+        size = len(starts) // 2
+        starts = starts[size * half : size * (half + 1)]
+    return jnp.concatenate([ref[k : k + height, :] for k in starts], axis=1)
+
+
 def slot_parts(owner_row, count):
     rows = owner_row.shape[1]
     hits = (iota((count, rows), 0) == owner_row).astype(F32)
@@ -99,9 +107,9 @@
 
 def send_kernel(
     corner_hbm, owner_hbm, vis_hbm, ku_hbm, kv_hbm, off_hbm, image_hbm,
-    send_ref, table_ref, hits_ref, rank_ref, corner_out, start_ref,
+    send_ref, hits_ref, rank_ref, corner_out, start_ref,
     corner_ref, owner_ref, vis_ref, ku_ref, kv_ref, off_ref, image_ref,
-    freq_ref, cos_ref, sin_ref, mod_ref, sem_ref, *, count, cap,
+    freq_ref, table_ref, mod_ref, sem_ref, *, count, cap,
 ):
     lane_groups, row_blocks, piece = layout_of(cap)
     sources = [corner_hbm, image_hbm, owner_hbm, vis_hbm, ku_hbm, kv_hbm, off_hbm, corner_hbm]
@@ -114,34 +122,31 @@
     facet = lax.axis_index("facet")
     x_start = facet % ACROSS * FACET - GRID // 2
     for at, cos_t, sin_t in phase_tiles(iota((SUB, LANES), 0)):
-        table_ref[:SUB, at : at + LANES] = cos_t.astype(BF16)
-        table_ref[SUB:, at : at + LANES] = sin_t.astype(BF16)
+        table_ref[at : at + SUB, :] = cos_t.astype(BF16)
+        table_ref[at + SUB : at + LANES, :] = sin_t.astype(BF16)
     copies[0].wait()
     start_ref[...] = jnp.full(start_ref.shape, corner_ref[1, facet], I32)
     for s in range(count):
         freq_ref[s : s + 1, :] = jnp.full((1, LANES), corner_ref[0, s], I32)
     freq = freq_ref[...]
-    for at, cos_u, sin_u in phase_tiles(freq):
-        cos_ref[:, at : at + LANES] = cos_u
-        sin_ref[:, at : at + LANES] = -sin_u
     for copy in copies[1:]:
         copy.wait()
-    image = image_ref[...]
-    for s in range(count):
-        both = jnp.concatenate([image * spread_row(cos_ref, s), image * spread_row(sin_ref, s)], axis=0)
-        mod_ref[16 * s : 16 * s + 16, :] = both.astype(BF16)
-    prod = dot_nt(mod_ref[...], table_ref[...])
-    lane = iota((FROWS, LANES), 1)
-    low = lane < SUB
+    for at, cos_u, sin_u in phase_tiles(freq):
+        for y in range(FROWS):
+            row = jnp.broadcast_to(image_ref[y : y + 1, at : at + LANES], (count, LANES))
+            start = 2 * count * (at // LANES * FROWS + y)
+            mod_ref[start : start + count, :] = (row * cos_u).astype(BF16)
+            mod_ref[start + count : start + 2 * count, :] = (row * -sin_u).astype(BF16)
+    prod = dot_nt(side_by_side(mod_ref, 2 * FROWS * count), side_by_side(table_ref, LANES))
+    low = iota(freq.shape, 1) < SUB
     cos_x, sin_x = phase_pair((freq + (iota(freq.shape, 1) & (SUB - 1))) * x_start)
-    sin_x = jnp.where(iota(freq.shape, 1) < SUB, sin_x, -sin_x)
-    for s in range(count):
-        real_p = prod[16 * s : 16 * s + 8]
-        imag_p = pltpu.roll(prod[16 * s + 8 : 16 * s + 16], SUB, 1)
+    sin_x = jnp.where(low, sin_x, -sin_x)
+    for y in range(FROWS):
+        start = 2 * count * y
+        real_p = prod[start : start + count]
+        imag_p = pltpu.roll(prod[start + count : start + 2 * count], SUB, 1)
         col = jnp.where(low, real_p + imag_p, imag_p - real_p)
-        send_ref[piece * s : piece * s + FROWS, :] = (
-            col * cos_x[s : s + 1] + pltpu.roll(col, SUB, 1) * sin_x[s : s + 1]
-        )
+        send_ref[pl.ds(y, count, stride=piece), :] = col * cos_x + pltpu.roll(col, SUB, 1) * sin_x
 
     owner_row = owner_ref[...]
     rows = owner_row.shape[1]
@@ -278,8 +283,9 @@
 
 
 def second_kernel(
-    all_ref, select_ref, own_ref, col_ref, ku_ref, kh_ref, vis_ref, back_ref, *, count, cap, groups, scale,
+    all_ref, select_ref, own_ref, col_ref, ku_ref, kh_ref, vis_ref, *rest, count, cap, groups, scale,
 ):
+    back_ref = rest[-1]
     lane_groups = LANES // cap
     height = col_ref.shape[0]
     total = groups * count
@@ -290,8 +296,13 @@
         for d in range(chunk):
             at = pl.multiple_of((part * chunk + d) * height, 8)
             blocks.append(split(all_ref[pl.ds(at, height), :]))
-        at = pl.multiple_of(part * chunk * LANES, LANES)
-        return carry + dot_nn(jnp.concatenate(blocks, axis=1), select_ref[pl.ds(at, chunk * LANES), :])
+        size = chunk // 2
+        halves = []
+        for half in range(2):
+            at = pl.multiple_of((2 * part + half) * size * LANES, LANES)
+            left = jnp.concatenate(blocks[size * half : size * (half + 1)], axis=1)
+            halves.append(dot_nn(left, select_ref[pl.ds(at, size * LANES), :]))
+        return carry + (halves[0] - halves[1])
 
     extra = jnp.zeros((2 * height, LANES), F32)
     if total == chunk:
@@ -317,12 +328,24 @@
             back_ref[at + 8 : at + 9, :] = back[j][tile : tile + 1]
 
 
-def prepare_kernel(*refs, count, groups):
+def side_of(index, total):
+    chunk = math.gcd(total, 32)
+    return jnp.where(index % chunk < chunk // 2, 1.0, -1.0)
+
+
+def in_eights(total, step):
+    def eight(part, carry):
+        for k in range(8):
+            step(part * 8 + k)
+        return carry
+
+    lax.fori_loop(0, total // 8, eight, 0)
+
+
+def select_kernel(*refs, count, groups):
     corner_ref, near_refs = refs[0], refs[1:groups]
-    cos_ref, sin_ref, cos_x_ref, sin_x_ref, select_ref, freq_ref = refs[groups:]
-    facet = lax.axis_index("facet")
-    x_start = facet % ACROSS * FACET - GRID // 2
-    u_start = corner_ref[0, facet]
+    select_ref = refs[groups]
+    u_start = corner_ref[0, lax.axis_index("facet")]
     row, col = iota((LANES, LANES), 0), iota((LANES, LANES), 1)
     same = (row < SUB) == (col < SUB)
     row_a, col_a = row & (SUB - 1), col & (SUB - 1)
@@ -331,56 +354,98 @@
     sign = jnp.where(col < SUB, 1.0, -1.0)
     half = GRID // 2
 
-    def fill(d, carry):
+    def fill(d):
         u_other = group_corner(corner_ref, near_refs, d // count, groups, d % count)
-        freq_ref[pl.ds(d, 1), :] = jnp.full((1, LANES), u_other, I32)
         ahead = ((u_start - u_other + half) & (GRID - 1)) - half
         mirror = (-u_start - u_other) & (GRID - 1)
         select = jnp.where(behind == ahead, 1.0, 0.0) + jnp.where(across == mirror, sign, 0.0)
+        select = select * side_of(d, groups * count)
         select_ref[pl.ds(pl.multiple_of(d * LANES, LANES), LANES), :] = select.astype(BF16)
-        return carry
-
-    lax.fori_loop(0, groups * count, fill, 0)
-    freq = freq_ref[...]
-    cos_x, sin_x = phase_pair((freq + (iota(freq.shape, 1) & (SUB - 1))) * x_start)
-    cos_x_ref[...] = cos_x
-    sin_x_ref[...] = jnp.where(iota(freq.shape, 1) < SUB, -sin_x, sin_x)
+
+    in_eights(groups * count, fill)
+
+
+def turn_kernel(*refs, count, groups):
+    corner_ref, near_refs = refs[0], refs[1:groups]
+    same_ref, cross_ref, table_ref, freq_ref = refs[groups:]
     total = groups * count
-    for at, cos_u, sin_u in phase_tiles(freq):
-        place = slice(at // CHUNK * total, (at // CHUNK + 1) * total), slice(at % CHUNK, at % CHUNK + LANES)
-        cos_ref[place] = cos_u
-        sin_ref[place] = -sin_u
+    x_start = lax.axis_index("facet") % ACROSS * FACET - GRID // 2
+    cos_a, sin_a = phase_pair(iota((SUB, LANES), 0) * iota((SUB, LANES), 1))
+    lane = iota((FROWS, LANES), 1)
+
+    def fill(d):
+        u_other = group_corner(corner_ref, near_refs, d // count, groups, d % count)
+        freq_ref[pl.ds(d, 1), :] = jnp.full((1, LANES), u_other, I32)
+        cos_u, sin_u = phase_pair(u_other * lane)
+        cos_u, sin_u = [jnp.concatenate([x] * (SUB // FROWS), axis=0) for x in (cos_u, sin_u)]
+        both = jnp.concatenate([cos_u * cos_a - sin_u * sin_a, -sin_u * cos_a - cos_u * sin_a], axis=0)
+        table_ref[pl.ds(pl.multiple_of(d * LANES, LANES), LANES), :] = both.astype(BF16)
+
+    in_eights(total, fill)
+    freq = freq_ref[...] + (iota((total, LANES), 1) & (SUB - 1))
+    low = iota((total, LANES), 1) < SUB
+    cos_x, sin_x = phase_pair(freq * x_start)
+    turn_c, turn_s = phase_pair(freq * LANES)
+    side = side_of(iota((total, LANES), 0), total)
+    cos_x, sin_x = cos_x * side, sin_x * side
+    for h in range(TURNS):
+        same_ref[pl.ds(h, total, stride=TURNS), :] = cos_x
+        cross_ref[pl.ds(h, total, stride=TURNS), :] = jnp.where(low, -sin_x, sin_x)
+        cos_x, sin_x = cos_x * turn_c - sin_x * turn_s, sin_x * turn_c + cos_x * turn_s
 
 
 def image_kernel(
-    got_ref, table_ref, cos_ref, sin_ref, cos_x_ref, sin_x_ref, hits_ref, rank_ref, image_ref,
-    out_ref, res_ref, left_ref, *, count, groups, cap, scale,
+    got_ref, same_ref, cross_ref, table_ref, hits_ref, rank_ref, image_ref,
+    out_ref, res_ref, flip_ref, left_ref, sum_ref, *, count, groups, cap, scale,
 ):
     total = groups * count
-    low = iota((FROWS, LANES), 1) < SUB
-    cos_x, sin_x = cos_x_ref[...], sin_x_ref[...]
-    for d in range(total):
-        block = got_ref[BACK * d : BACK * d + 8, :]
-        moved = block * cos_x[d : d + 1] + pltpu.roll(block, SUB, 1) * sin_x[d : d + 1]
-        both = jnp.concatenate([jnp.where(low, moved, -moved), pltpu.roll(moved, SUB, 1)], axis=0)
-        left_ref[16 * d : 16 * d + 16, :] = both.astype(BF16)
-    for at in range(0, FACET, CHUNK):
-        cut = slice(at, at + CHUNK)
-        both = dot_nn(left_ref[...], table_ref[:, cut])
-        dirty = jnp.zeros((FROWS, CHUNK), F32)
-        for d in range(total):
-            row = at // CHUNK * total + d
-            dirty = dirty + both[16 * d : 16 * d + 8] * spread_row(cos_ref, row)
-            dirty = dirty + both[16 * d + 8 : 16 * d + 16] * spread_row(sin_ref, row)
-        out_ref[:, cut] = image_ref[:, cut] + (GAIN_STEP * scale) * dirty
+    chunk = math.gcd(total, 32)
+
+    def gather(part, carry):
+        for s in range(chunk):
+            d = part * chunk + s
+            block = got_ref[pl.ds(BACK * d, FROWS), :]
+            flip_ref[FROWS * s : FROWS * (s + 1), :] = pltpu.roll(block, SUB, 1)
+            near = pl.ds(pl.multiple_of(d * TURNS, TURNS), TURNS)
+            same, cross = same_ref[near, :], cross_ref[near, :]
+            for y in range(FROWS):
+                straight = jnp.broadcast_to(block[y : y + 1], (FROWS, LANES))
+                flipped = spread_row(flip_ref, FROWS * s + y)
+                parts = [
+                    straight * same[k : k + FROWS] + flipped * cross[k : k + FROWS]
+                    for k in range(0, TURNS, FROWS)
+                ]
+                start = TURNS * (FROWS * s + y)
+                left_ref[start : start + TURNS, :] = jnp.concatenate(parts, axis=0).astype(BF16)
+        halves = []
+        for half in range(2):
+            size = chunk // 2 * LANES
+            at = pl.multiple_of((2 * part + half) * size, LANES)
+            left = side_by_side(left_ref, FROWS * TURNS, half)
+            halves.append(dot_nn(left, table_ref[pl.ds(at, size), :]))
+        return carry + (halves[0] - halves[1])
+
+    dirty = jnp.zeros((FROWS * TURNS, LANES), F32)
+    if total == chunk:
+        dirty = gather(0, dirty)
+    else:
+        dirty = lax.fori_loop(0, total // chunk, gather, dirty)
+    sum_ref[...] = dirty
+    for h in range(TURNS):
+        cut = slice(h * LANES, (h + 1) * LANES)
+        out_ref[:, cut] = image_ref[:, cut] + (GAIN_STEP * scale) * sum_ref[pl.ds(h, FROWS, stride=TURNS), :]
 
     rows = rank_ref.shape[1]
     first = lax.axis_index("freq") * (count * BACK) + 8
     back = jnp.concatenate([got_ref[pl.ds(first + BACK * s, 1), :] for s in range(count)], axis=0)
+    high = split(back)
+    low = split(back - high[:count].astype(F32) - high[count:].astype(F32))
+    back = jnp.concatenate([high, low[:count]], axis=0)
     picked = []
     for part in range(2):
-        place = (iota((LANES, rows), 0) == rank_ref[...] + part * cap).astype(F32)
-        found = dot_nn(back, place, exact_products)
+        place = (iota((LANES, rows), 0) == rank_ref[...] + part * cap).astype(F32).astype(BF16)
+        found = dot_nn(back, place)
+        found = found[:count] + found[count : 2 * count] + found[2 * count :]
         picked.append(jnp.sum(found * hits_ref[...], axis=0, keepdims=True))
     res_ref[...] = jnp.concatenate(picked, axis=0)
 
@@ -422,11 +487,10 @@
         return lax.all_to_all(view, axes, split_axis=0, concat_axis=0, tiled=True).reshape(block.shape)
 
     inputs = [corner, owner_row, visibilities, kernel_u, kernel_v, offsets, model_image]
-    send, table, hits, rank, corner, start = call(
+    send, hits, rank, corner, start = call(
         send_kernel,
         (
             shape(count * piece, LANES),
-            shape(2 * SUB, FACET, dtype=BF16),
             shape(count, rows),
             shape(1, rows, dtype=I32),
             shape(*corner.shape, dtype=I32),
@@ -439,9 +503,8 @@
         + [pltpu.VMEM(x.shape, x.dtype) for x in inputs[1:]]
         + [
             pltpu.VMEM((count, LANES), I32),
-            pltpu.VMEM((count, FACET), F32),
-            pltpu.VMEM((count, FACET), F32),
-            pltpu.VMEM((16 * count, FACET), BF16),
+            pltpu.VMEM((FACET, LANES), BF16),
+            pltpu.VMEM((2 * FROWS * count * TURNS, LANES), BF16),
             pltpu.SemaphoreType.DMA((8,)),
         ],
         far,
@@ -472,41 +535,60 @@
         scale=scale,
     )
     everyone = exchange(spread, ("freq", "facet"), total)
-    *phases, select = call(
-        prepare_kernel,
-        (
-            shape(FACET // CHUNK * total, CHUNK),
-            shape(FACET // CHUNK * total, CHUNK),
-            shape(total, LANES),
-            shape(total, LANES),
-            shape(total * LANES, LANES, dtype=BF16),
-        ),
+    select = call(
+        select_kernel,
+        shape(total * LANES, LANES, dtype=BF16),
         [corner, *near],
         [],
-        "prepare",
-        [pltpu.VMEM((total, LANES), I32)],
+        "overlaps",
         count=count,
         groups=groups,
     )
+
+    def make_turns(corner):
+        return call(
+            turn_kernel,
+            (
+                shape(total * TURNS, LANES),
+                shape(total * TURNS, LANES),
+                shape(total * LANES, LANES, dtype=BF16),
+            ),
+            [corner, *near],
+            [],
+            "turns",
+            [pltpu.VMEM((total, LANES), I32)],
+            count=count,
+            groups=groups,
+        )
+
+    early = total <= 64
+    turns = make_turns(corner) if early else ()
     back = call(
         second_kernel,
         shape(total * BACK, LANES),
         [],
-        [everyone, select, own, columns, kern_u, kern_h, vis],
+        [everyone, select, own, columns, kern_u, kern_h, vis, *turns[:1]],
         "second_cycle",
         count=count,
         cap=cap,
         groups=groups,
         scale=scale,
     )
+    if not early:
+        back, corner = lax.optimization_barrier((back, corner))
+        turns = make_turns(corner)
     returned = exchange(back, ("freq", "facet"), total)
     return call(
         image_kernel,
         (shape(FROWS, FACET), shape(2, rows)),
         [],
-        [returned, table, *phases, hits, rank, model_image],
+        [returned, *turns, hits, rank, model_image],
         "form_image",
-        [pltpu.VMEM((16 * total, LANES), BF16)],
+        [
+            pltpu.VMEM((FROWS * math.gcd(total, 32), LANES), F32),
+            pltpu.VMEM((FROWS * TURNS * math.gcd(total, 32), LANES), BF16),
+            pltpu.VMEM((FROWS * TURNS, LANES), F32),
+        ],
         count=count,
         groups=groups,
         cap=cap,

time: 46.5 us -> 46.2 us (level)
  waiting for transfers between devices: 6.75 us -> 5.72 us
  Pallas kernels: 7.12 us -> 7.9 us
    all_to_all x1, waiting for transfers between devices: 4.77 us -> 3.75 us  [exchange(): lax.all_to_all(view, axes, split_axis=0, concat_axis=0, tiled=True)]
    pallas_call x5 -> x6, Pallas kernels: 7.12 us -> 7.9 us  [call(): pl.pallas_call(lambda *refs: body(*refs, **sizes), out_shape=out_shape, i...]
  transfers between devices with their start and end apart: 2 -> 2, of which waited for: 2 -> 2; matrix products, arithmetic and copies ran while one was open for 0% -> 0% of each run, Pallas kernels for 4% -> 6%
where the time goes in v5:
time: 46.2 us; the launch traced here: 45.9 us
  blocking collectives  27.2 us (59%)
  Pallas kernels  7.9 us (17%)
  waiting for transfers between devices  5.72 us (12%)
  starting transfers between devices  4.42 us (10%)
  between operations  0.68 us (1%)
    all_to_all x2, blocking collectives, exchange(): lax.all_to_all(view, axes, split_axis=0, concat_axis=0, tiled=True)  27.2 us
    pallas_call x6, Pallas kernels, call(): pl.pallas_call(lambda *refs: body(*refs, **sizes), out_shape=out_shape, i...  7.9 us
    all_to_all x1, waiting for transfers between devices, exchange(): lax.all_to_all(view, axes, split_axis=0, concat_axis=0, tiled=True)  3.75 us
    all_to_all x1, starting transfers between devices, exchange(): lax.all_to_all(view, axes, split_axis=0, concat_axis=0, tiled=True)  2.59 us
    ppermute x1, waiting for transfers between devices, on_device(): lax.ppermute(corner, 'freq', [(g, (g + k) % groups) for g in range(groups)])  1.97 us
    ppermute x1, starting transfers between devices, on_device(): lax.ppermute(corner, 'freq', [(g, (g + k) % groups) for g in range(groups)])  1.82 us
  transfers between devices with their start and end apart: 2, of which 2 were waited for; matrix products, arithmetic and copies ran while one was open for 0% of the time, Pallas kernels for 6%

profile of v5, /device:TPU:0, one launch (start us, length us, event | category | flops | bytes accessed | tf_op | source)
XLA Modules:
  0.0 45.9 jit_solution(4059187565411667170)
XLA Ops:
  0.6 1.7 %send_rows.1 = (f32[416,128]{1,0:T(8,128)S(1)}, f32[16,256]{1,0:T(8,128)S(1)}, s32[1,256]{1,0:T(1,128)S(1)}, s32[2,16]{1,0:T(2,128)S(1)}, s32[8,128]{1,0:T(8,128)S(1)}) custom-call(s32[2,16]{1,0:T(2,128)} %bitcast.15, s32[1,256]{1,0:T(1,128)} %bitcast.16, f32[2,256]{1,0:T(2,128)} %refs_2_.1, f32[16,256]{1,0:T(8,128)} %refs_3_.1, f32[16,256]{1,0:T(8,128)} %refs_4_.1, ...), custom_call_target="tpu_custom_call" | custom-call | tf_op jit(solution)/shard_map/send_rows/pallas_call | solution.py:475
  2.4 16.4 %all_to_all.15 = f32[16,1,3328]{2,1,0:T(1,128)S(1)} all-to-all(f32[16,1,3328]{2,1,0:T(1,128)S(1)} %bitcast.14), channel_id=1, replica_groups=mesh['freq'=2,'facet'=16] {'facet'}, dimensions={0} | all-to-all | bytes 425984 | tf_op jit(solution)/shard_map/all_to_all | solution.py:487
  18.8 1.4 %first_cycle.1 = (f32[16,128]{1,0:T(8,128)S(1)}, bf16[128,1024]{1,0:T(8,128)(2,1)S(1)}, f32[32,1024]{1,0:T(8,128)S(1)}, f32[2,1024]{1,0:T(2,128)S(1)}, f32[512,128]{1,0:T(8,128)}, /*index=5*/f32[16,128]{1,0:T(8,128)S(1)}) custom-call(s32[8,128]{1,0:T(8,128)S(1)} %get-tuple-element.16.refs_0_, f32[416,128]{1,0:T(8,128)S(1)} %bitcast.11), custom_call_target="tpu_custom_call" | custom-call | tf_op jit(solution)/shard_map/first_cycle/pallas_call | solution.py:475
  20.2 2.6 %all-to-all-start.1 = ((f32[32,1,2048]{2,1,0:T(1,128)}), f32[32,1,2048]{2,1,0:T(1,128)S(1)}, u32[]{:S(2)}, u32[]{:S(2)}) async-start(f32[32,1,2048]{2,1,0:T(1,128)} %bitcast.5), calls=%async_computation.1 | async-start | bytes 524288 | tf_op jit(solution)/shard_map/all_to_all | solution.py:487
  22.8 1.8 %collective-permute-start = (s32[2,16]{1,0:T(2,128)S(1)}, s32[2,16]{1,0:T(2,128)S(1)}, u32[]{:S(2)}, u32[]{:S(2)}) collective-permute-start(s32[2,16]{1,0:T(2,128)S(1)} %get-tuple-element.19.refs_0_), channel_id=1, source_target_pairs={{0,16},{16,0},{1,17},{17,1},{2,18},{18,2},{3,19},{19,3},{4,20},{20... | collective-permute-start | bytes 392 | tf_op jit(solution)/shard_map/ppermute | solution.py:515
  24.7 2.0 %collective-permute-done.refs_1_ = s32[2,16]{1,0:T(2,128)S(1)} collective-permute-done((s32[2,16]{1,0:T(2,128)S(1)}, s32[2,16]{1,0:T(2,128)S(1)}, u32[]{:S(2)}, u32[]{:S(2)}) %collective-permute-start) | collective-permute-done | bytes 160 | tf_op jit(solution)/shard_map/ppermute | solution.py:515
  26.6 1.3 %overlaps.1.refs_1_ = bf16[4096,128]{1,0:T(8,128)(2,1)S(1)} custom-call(s32[2,16]{1,0:T(2,128)S(1)} %get-tuple-element.19.refs_0_, s32[2,16]{1,0:T(2,128)S(1)} %collective-permute-done.refs_1_), custom_call_target="tpu_custom_call" | custom-call | tf_op jit(solution)/shard_map/overlaps/pallas_call | solution.py:475
  27.9 1.4 %turns.1 = (f32[512,128]{1,0:T(8,128)S(1)}, f32[512,128]{1,0:T(8,128)S(1)}, bf16[4096,128]{1,0:T(8,128)(2,1)S(1)}) custom-call(s32[2,16]{1,0:T(2,128)S(1)} %get-tuple-element.19.refs_0_, s32[2,16]{1,0:T(2,128)S(1)} %collective-permute-done.refs_1_), custom_call_target="tpu_custom_call" | custom-call | tf_op jit(solution)/shard_map/turns/pallas_call | solution.py:475
  29.3 3.8 %all-to-all-done.1 = f32[32,1,2048]{2,1,0:T(1,128)S(1)} async-done(((f32[32,1,2048]{2,1,0:T(1,128)}), f32[32,1,2048]{2,1,0:T(1,128)S(1)}, u32[]{:S(2)}, u32[]{:S(2)}) %all-to-all-start.1) | async-done | bytes 262176 | tf_op jit(solution)/shard_map/all_to_all | solution.py:487
  33.1 0.8 %second_cycle.1 = f32[288,128]{1,0:T(8,128)S(1)} custom-call(f32[512,128]{1,0:T(8,128)S(1)} %bitcast.10, bf16[4096,128]{1,0:T(8,128)(2,1)S(1)} %overlaps.1.refs_1_, f32[16,128]{1,0:T(8,128)S(1)} %get-tuple-element.20.refs_2_, f32[16,128]{1,0:T(8,128)S(1)} %get-tuple-element.21.refs_3_, bf16[128,1024]{1,0:T(8,128)(2,1)S(1)} %get-tuple-element.22.refs_4_, ...), custom_call_target="tpu_custom_call" | custom-call | tf_op jit(solution)/shard_map/second_cycle/pallas_call | solution.py:475
  33.9 0.0 copy-start
  33.9 10.8 %all_to_all.16 = f32[32,1,1152]{2,1,0:T(1,128)S(1)} all-to-all(f32[32,1,1152]{2,1,0:T(1,128)S(1)} %bitcast.13), channel_id=1, replica_groups=mesh['freq'=2,'facet'=16] {'freq','facet'}, dimensions={0} | all-to-all | bytes 294912 | tf_op jit(solution)/shard_map/all_to_all | solution.py:487
  44.6 0.0 copy-done
  44.6 1.3 %form_image.1 = (f32[8,2048]{1,0:T(8,128)}, f32[2,256]{1,0:T(2,128)}) custom-call(f32[288,128]{1,0:T(8,128)S(1)} %bitcast.12, f32[512,128]{1,0:T(8,128)S(1)} %get-tuple-element.25.refs_7_.refs_1_, f32[512,128]{1,0:T(8,128)S(1)} %get-tuple-element.26.refs_2_, bf16[4096,128]{1,0:T(8,128)(2,1)S(1)} %get-tuple-element.27.refs_3_, ...), custom_call_target="tpu_custom_call" | custom-call | tf_op jit(solution)/shard_map/form_image/pallas_call | solution.py:475
Async XLA Ops:
  20.2 12.9 %all-to-all-start.1 = ((f32[32,1,2048]{2,1,0:T(1,128)}), f32[32,1,2048]{2,1,0:T(1,128)S(1)}, u32[]{:S(2)}, u32[]{:S(2)}) async-start(f32[32,1,2048]{2,1,0:T(1,128)} %bitcast.5), calls=%async_computation.1 | async-start | bytes 524288 | tf_op jit(solution)/shard_map/all_to_all | solution.py:487
  22.8 3.8 %collective-permute-start = (s32[2,16]{1,0:T(2,128)S(1)}, s32[2,16]{1,0:T(2,128)S(1)}, u32[]{:S(2)}, u32[]{:S(2)}) collective-permute-start(s32[2,16]{1,0:T(2,128)S(1)} %get-tuple-element.19.refs_0_), channel_id=1, source_target_pairs={{0,16},{16,0},{1,17},{17,1},{2,18},{18,2},{3,19},{19,3},{4,20},{20... | collective-permute-start | bytes 392 | tf_op jit(solution)/shard_map/ppermute | solution.py:515
  33.9 10.8 %copy-start = (f32[8,2048]{1,0:T(8,128)S(1)}, f32[8,2048]{1,0:T(8,128)}, u32[]{:S(2)}) copy-start(f32[8,2048]{1,0:T(8,128)} %refs_6_.3) | copy-start | bytes 196612
